TPU v7x, 32 devices: a whole 2x2x4 slice. The times are simulated.
32 devices in a mesh: pgrp: 4 (over y, core), srow: 8 (over z, x).
Axes of the slice: x: 2, y: 2, z: 4, core: 2. Of those that a mesh axis runs over, the one named last changes fastest.
Arguments:
- kernel: bfloat16 [608, 224, 512], P('srow', None, 'pgrp'), may hold values from -0.0234375 to 0.0234375
- probes: bfloat16 [4, 608, 224], P(None, 'srow', 'pgrp'), may hold values from -6 to 6
- prior_var: float32 [512], P('pgrp'), may hold values from 0.3 to 3
- noise_var: float32 [608], P('srow'), may hold values from 0.1 to 1
Outputs:
- hessian_probes: float32 [4, 608, 224], P(None, 'srow', 'pgrp')
All inputs are finite; a program needn't handle non-finite values.
Results may differ from a plain program's by a relative error of at most 0.0022.
Values may be sent and summed in bfloat16 or wider, within the bound.
No kernel may reach another device: no remote copies, remote signals or barrier semaphores. Data moves between devices by JAX's collectives and lax.ppermute only.
A program may use at most 64 MiB of HBM per device.

v0:
```python
import math

import jax
import jax.numpy as jnp
from jax import lax
from jax.sharding import PartitionSpec as P


def lag_block(length):
    return math.gcd(length, 28)


def correlate(series, kernel):
    length = series.shape[2]
    width = lag_block(length)
    padded = jnp.concatenate([series, jnp.zeros_like(series)], axis=2)
    offsets = jnp.arange(width, dtype=jnp.int32)

    def correlate_one_turn(turn, total):
        first = (turn * width).astype(jnp.int32)

        def correlate_shifted(offset):
            return lax.dynamic_slice_in_dim(padded, first + offset, length, 2)

        window = jax.vmap(correlate_shifted, out_axes=2)(offsets)
        kernel_part = lax.dynamic_slice_in_dim(kernel, first, width, 1)
        return total + jnp.einsum(
            "sjp,nsjt->npt", kernel_part, window, preferred_element_type=jnp.float32
        )

    start = jnp.zeros((series.shape[0], kernel.shape[2], length), jnp.float32)
    return lax.fori_loop(0, length // width, correlate_one_turn, start)


def convolve(params, kernel):
    length = params.shape[2]
    width = lag_block(length)
    padded = jnp.concatenate([jnp.zeros_like(params), params], axis=2)
    offsets = jnp.arange(width, dtype=jnp.int32)

    def convolve_one_turn(turn, total):
        first = (turn * width).astype(jnp.int32)

        def convolve_shifted(offset):
            return lax.dynamic_slice_in_dim(padded, length - first - offset, length, 2)

        window = jax.vmap(convolve_shifted, out_axes=2)(offsets)
        kernel_part = lax.dynamic_slice_in_dim(kernel, first, width, 1)
        return total + jnp.einsum(
            "sjp,npjt->nst", kernel_part, window, preferred_element_type=jnp.float32
        )

    start = jnp.zeros((params.shape[0], kernel.shape[0], length), jnp.float32)
    return lax.fori_loop(0, length // width, convolve_one_turn, start)


def on_device(kernel, probes, prior_var, noise_var):
    series = lax.all_gather(probes, "pgrp", axis=2, tiled=True)
    adjoint = correlate(series, kernel)
    totals = lax.psum(adjoint, "srow")
    params = (totals * prior_var[None, :, None]).astype(jnp.bfloat16)
    forward = convolve(params, kernel)
    summed = lax.psum_scatter(forward, "pgrp", scatter_dimension=2, tiled=True)
    return summed + noise_var[None, :, None] * probes.astype(jnp.float32)


def solution(mesh):
    placed = (P("srow", None, "pgrp"), P(None, "srow", "pgrp"), P("pgrp"), P("srow"))
    return jax.shard_map(
        on_device, mesh=mesh, in_specs=placed, out_specs=P(None, "srow", "pgrp"), check_vma=False
    )
```

profile of v0, /device:TPU:0, one launch (start us, length us, event | category | flops | bytes accessed | tf_op | source)
XLA Modules:
  0.0 345.0 jit_solution(17294835956913553956)
XLA Ops:
  6.5 6.1 %copy.15 = bf16[76,224,128]{2,0,1:T(8,128)(2,1)} copy(bf16[76,224,128]{2,1,0:T(8,128)(2,1)} %param.8) | data formatting | bytes 8716288
  12.7 7.1 %all_gather.3 = bf16[4,76,224]{1,0,2:T(4,128)(2,1)S(1)} all-gather(bf16[4,76,56]{1,0,2:T(4,128)(2,1)S(1)} %copy.14), channel_id=1, replica_groups=mesh['pgrp'=4,'srow'=8] {'pgrp'}, dimensions={2}, use_global_device_ids=true | all-gather | bytes 170240 | tf_op jit(solution)/shard_map/all_gather | solution.py:58
  19.8 0.2 concatenate.16
  20.0 0.0 copy-start.1
  20.0 107.9 %while.28 = (s32[]{:T(128)}, f32[4,128,224]{1,2,0:T(8,128)S(1)}, bf16[4,76,448]{1,0,2:T(4,128)(2,1)S(1)}, bf16[76,224,128]{2,0,1:T(8,128)(2,1)}, s32[]{:T(128)}, /*index=5*/s32[]{:T(128)}, s32[]{:T(128)}, s32[]{:T(128)}) while((s32[]{:T(128)}, f32[4,128,224]{1,2,0:T(8,128)S(1)}, bf16[4,76,448]{1,0,2:T(4,128)(2,1)S(1)}, ...), condition=%wide.region_1.0_spmd.clone, body=%wide.region_0.0_spmd.clone.sunk | while | flops 488341664 | bytes 15540821 | solution.py:32
  20.0 8.8 %gather_fusion = bf16[28,4,76,224]{2,1,3,0:T(4,128)(2,1)} fusion(bf16[4,76,448]{1,0,2:T(4,128)(2,1)S(1)} %get-tuple-element.329, s32[28]{0:T(128)S(1)} %fusion.42), kind=kCustom, calls=%fused_computation.clone.clone.1 | custom fusion | bytes 7627088 | tf_op jit(solution)/shard_map/while/body/eval_jaxpr/vmap()/gather | solution.py:23
  28.8 4.7 %fusion.43 = f32[4,128,224]{1,2,0:T(8,128)S(1)} fusion(bf16[4,76,28,224]{1,0,3,2:T(4,128)(2,1)} %bitcast.51, bf16[76,224,128]{2,0,1:T(8,128)(2,1)} %get-tuple-element.330, s32[]{:T(128)S(6)} %select_n.65, f32[4,128,224]{1,2,0:T(8,128)S(1)} %get-tuple-element.320, pred[]{:T(512)S(6)} %compare.10), kind=kOutput, calls=%fused_computation.7.clone.1 | convolution fusion | flops 488341504 | bytes 7913477 | tf_op jit(solution)/shard_map/while/body/eval_jaxpr/sjp,nsjt->npt/dot_general | solution.py:27
  33.5 8.8 %gather_fusion = bf16[28,4,76,224]{2,1,3,0:T(4,128)(2,1)} fusion(bf16[4,76,448]{1,0,2:T(4,128)(2,1)S(1)} %get-tuple-element.329, s32[28]{0:T(128)S(1)} %fusion.42), kind=kCustom, calls=%fused_computation.clone.clone.1 | custom fusion | bytes 7627088 | tf_op jit(solution)/shard_map/while/body/eval_jaxpr/vmap()/gather | solution.py:23
  42.3 4.7 %fusion.43 = f32[4,128,224]{1,2,0:T(8,128)S(1)} fusion(bf16[4,76,28,224]{1,0,3,2:T(4,128)(2,1)} %bitcast.51, bf16[76,224,128]{2,0,1:T(8,128)(2,1)} %get-tuple-element.330, s32[]{:T(128)S(6)} %select_n.65, f32[4,128,224]{1,2,0:T(8,128)S(1)} %get-tuple-element.320, pred[]{:T(512)S(6)} %compare.10), kind=kOutput, calls=%fused_computation.7.clone.1 | convolution fusion | flops 488341504 | bytes 7913477 | tf_op jit(solution)/shard_map/while/body/eval_jaxpr/sjp,nsjt->npt/dot_general | solution.py:27
  47.0 8.8 %gather_fusion = bf16[28,4,76,224]{2,1,3,0:T(4,128)(2,1)} fusion(bf16[4,76,448]{1,0,2:T(4,128)(2,1)S(1)} %get-tuple-element.329, s32[28]{0:T(128)S(1)} %fusion.42), kind=kCustom, calls=%fused_computation.clone.clone.1 | custom fusion | bytes 7627088 | tf_op jit(solution)/shard_map/while/body/eval_jaxpr/vmap()/gather | solution.py:23
  55.8 4.7 %fusion.43 = f32[4,128,224]{1,2,0:T(8,128)S(1)} fusion(bf16[4,76,28,224]{1,0,3,2:T(4,128)(2,1)} %bitcast.51, bf16[76,224,128]{2,0,1:T(8,128)(2,1)} %get-tuple-element.330, s32[]{:T(128)S(6)} %select_n.65, f32[4,128,224]{1,2,0:T(8,128)S(1)} %get-tuple-element.320, pred[]{:T(512)S(6)} %compare.10), kind=kOutput, calls=%fused_computation.7.clone.1 | convolution fusion | flops 488341504 | bytes 7913477 | tf_op jit(solution)/shard_map/while/body/eval_jaxpr/sjp,nsjt->npt/dot_general | solution.py:27
  60.5 8.8 %gather_fusion = bf16[28,4,76,224]{2,1,3,0:T(4,128)(2,1)} fusion(bf16[4,76,448]{1,0,2:T(4,128)(2,1)S(1)} %get-tuple-element.329, s32[28]{0:T(128)S(1)} %fusion.42), kind=kCustom, calls=%fused_computation.clone.clone.1 | custom fusion | bytes 7627088 | tf_op jit(solution)/shard_map/while/body/eval_jaxpr/vmap()/gather | solution.py:23
  69.3 4.7 %fusion.43 = f32[4,128,224]{1,2,0:T(8,128)S(1)} fusion(bf16[4,76,28,224]{1,0,3,2:T(4,128)(2,1)} %bitcast.51, bf16[76,224,128]{2,0,1:T(8,128)(2,1)} %get-tuple-element.330, s32[]{:T(128)S(6)} %select_n.65, f32[4,128,224]{1,2,0:T(8,128)S(1)} %get-tuple-element.320, pred[]{:T(512)S(6)} %compare.10), kind=kOutput, calls=%fused_computation.7.clone.1 | convolution fusion | flops 488341504 | bytes 7913477 | tf_op jit(solution)/shard_map/while/body/eval_jaxpr/sjp,nsjt->npt/dot_general | solution.py:27
  74.0 8.8 %gather_fusion = bf16[28,4,76,224]{2,1,3,0:T(4,128)(2,1)} fusion(bf16[4,76,448]{1,0,2:T(4,128)(2,1)S(1)} %get-tuple-element.329, s32[28]{0:T(128)S(1)} %fusion.42), kind=kCustom, calls=%fused_computation.clone.clone.1 | custom fusion | bytes 7627088 | tf_op jit(solution)/shard_map/while/body/eval_jaxpr/vmap()/gather | solution.py:23
  82.8 4.7 %fusion.43 = f32[4,128,224]{1,2,0:T(8,128)S(1)} fusion(bf16[4,76,28,224]{1,0,3,2:T(4,128)(2,1)} %bitcast.51, bf16[76,224,128]{2,0,1:T(8,128)(2,1)} %get-tuple-element.330, s32[]{:T(128)S(6)} %select_n.65, f32[4,128,224]{1,2,0:T(8,128)S(1)} %get-tuple-element.320, pred[]{:T(512)S(6)} %compare.10), kind=kOutput, calls=%fused_computation.7.clone.1 | convolution fusion | flops 488341504 | bytes 7913477 | tf_op jit(solution)/shard_map/while/body/eval_jaxpr/sjp,nsjt->npt/dot_general | solution.py:27
  87.5 8.8 %gather_fusion = bf16[28,4,76,224]{2,1,3,0:T(4,128)(2,1)} fusion(bf16[4,76,448]{1,0,2:T(4,128)(2,1)S(1)} %get-tuple-element.329, s32[28]{0:T(128)S(1)} %fusion.42), kind=kCustom, calls=%fused_computation.clone.clone.1 | custom fusion | bytes 7627088 | tf_op jit(solution)/shard_map/while/body/eval_jaxpr/vmap()/gather | solution.py:23
  96.2 4.7 %fusion.43 = f32[4,128,224]{1,2,0:T(8,128)S(1)} fusion(bf16[4,76,28,224]{1,0,3,2:T(4,128)(2,1)} %bitcast.51, bf16[76,224,128]{2,0,1:T(8,128)(2,1)} %get-tuple-element.330, s32[]{:T(128)S(6)} %select_n.65, f32[4,128,224]{1,2,0:T(8,128)S(1)} %get-tuple-element.320, pred[]{:T(512)S(6)} %compare.10), kind=kOutput, calls=%fused_computation.7.clone.1 | convolution fusion | flops 488341504 | bytes 7913477 | tf_op jit(solution)/shard_map/while/body/eval_jaxpr/sjp,nsjt->npt/dot_general | solution.py:27
  100.9 8.8 %gather_fusion = bf16[28,4,76,224]{2,1,3,0:T(4,128)(2,1)} fusion(bf16[4,76,448]{1,0,2:T(4,128)(2,1)S(1)} %get-tuple-element.329, s32[28]{0:T(128)S(1)} %fusion.42), kind=kCustom, calls=%fused_computation.clone.clone.1 | custom fusion | bytes 7627088 | tf_op jit(solution)/shard_map/while/body/eval_jaxpr/vmap()/gather | solution.py:23
  109.7 4.7 %fusion.43 = f32[4,128,224]{1,2,0:T(8,128)S(1)} fusion(bf16[4,76,28,224]{1,0,3,2:T(4,128)(2,1)} %bitcast.51, bf16[76,224,128]{2,0,1:T(8,128)(2,1)} %get-tuple-element.330, s32[]{:T(128)S(6)} %select_n.65, f32[4,128,224]{1,2,0:T(8,128)S(1)} %get-tuple-element.320, pred[]{:T(512)S(6)} %compare.10), kind=kOutput, calls=%fused_computation.7.clone.1 | convolution fusion | flops 488341504 | bytes 7913477 | tf_op jit(solution)/shard_map/while/body/eval_jaxpr/sjp,nsjt->npt/dot_general | solution.py:27
  114.4 8.8 %gather_fusion = bf16[28,4,76,224]{2,1,3,0:T(4,128)(2,1)} fusion(bf16[4,76,448]{1,0,2:T(4,128)(2,1)S(1)} %get-tuple-element.329, s32[28]{0:T(128)S(1)} %fusion.42), kind=kCustom, calls=%fused_computation.clone.clone.1 | custom fusion | bytes 7627088 | tf_op jit(solution)/shard_map/while/body/eval_jaxpr/vmap()/gather | solution.py:23
  123.2 4.7 %fusion.43 = f32[4,128,224]{1,2,0:T(8,128)S(1)} fusion(bf16[4,76,28,224]{1,0,3,2:T(4,128)(2,1)} %bitcast.51, bf16[76,224,128]{2,0,1:T(8,128)(2,1)} %get-tuple-element.330, s32[]{:T(128)S(6)} %select_n.65, f32[4,128,224]{1,2,0:T(8,128)S(1)} %get-tuple-element.320, pred[]{:T(512)S(6)} %compare.10), kind=kOutput, calls=%fused_computation.7.clone.1 | convolution fusion | flops 488341504 | bytes 7913477 | tf_op jit(solution)/shard_map/while/body/eval_jaxpr/sjp,nsjt->npt/dot_general | solution.py:27
  127.9 1.1 copy.16
  129.0 0.0 all-reduce.6.cloned.1.call-update
  129.0 0.2 reduce-scatter.2.cloned.1.call-start
  129.2 73.5 %all-reduce.6.cloned.1.call-done = f32[4,128,224]{1,0,2:T(4,128)} async-done(((f32[4,128,224]{1,0,2:T(4,128)}), f32[4,128,224]{1,0,2:T(4,128)}) %all-reduce.6.cloned.1.call-update) | async-done | bytes 458768 | tf_op jit(solution)/shard_map/psum | solution.py:60
  202.8 1.1 multiply_convert_fusion
  203.9 0.1 concatenate.17
  204.0 110.9 %while.29 = (s32[]{:T(128)}, f32[4,76,224]{2,1,0:T(8,128)S(1)}, bf16[4,128,448]{1,0,2:T(4,128)(2,1)S(1)}, bf16[76,224,128]{2,0,1:T(8,128)(2,1)}, s32[]{:T(128)}, /*index=5*/s32[]{:T(128)}, s32[]{:T(128)}, s32[]{:T(128)}) while((s32[]{:T(128)}, f32[4,76,224]{2,1,0:T(8,128)S(1)}, bf16[4,128,448]{1,0,2:T(4,128)(2,1)S(1)}, ...), condition=%wide.region_4.0_spmd.clone, body=%wide.region_3.0_spmd.clone.sunk | while | flops 488248480 | bytes 20386400 | solution.py:54
  204.1 8.8 %gather_fusion.1 = bf16[28,4,128,224]{2,1,3,0:T(4,128)(2,1)} fusion(bf16[4,128,448]{1,0,2:T(4,128)(2,1)S(1)} %get-tuple-element.353, s32[28]{0:T(128)S(1)} %fusion.46), kind=kCustom, calls=%fused_computation.1.clone.clone.1 | custom fusion | bytes 12845392 | tf_op jit(solution)/shard_map/while/body/eval_jaxpr/vmap()/gather | solution.py:45
  212.9 5.0 %fusion.47 = f32[4,76,224]{2,1,0:T(8,128)S(1)} fusion(bf16[4,128,28,224]{1,0,3,2:T(4,128)(2,1)} %bitcast.50, bf16[76,224,128]{2,0,1:T(8,128)(2,1)} %get-tuple-element.354, s32[]{:T(128)S(6)} %select_n.67, f32[4,76,224]{2,1,0:T(8,128)S(1)} %get-tuple-element.344, pred[]{:T(512)S(6)} %compare.11), kind=kOutput, calls=%fused_computation.19.clone.1 | convolution fusion | flops 488248320 | bytes 7540741 | tf_op jit(solution)/shard_map/while/body/eval_jaxpr/sjp,npjt->nst/dot_general | solution.py:49
  217.9 8.8 %gather_fusion.1 = bf16[28,4,128,224]{2,1,3,0:T(4,128)(2,1)} fusion(bf16[4,128,448]{1,0,2:T(4,128)(2,1)S(1)} %get-tuple-element.353, s32[28]{0:T(128)S(1)} %fusion.46), kind=kCustom, calls=%fused_computation.1.clone.clone.1 | custom fusion | bytes 12845392 | tf_op jit(solution)/shard_map/while/body/eval_jaxpr/vmap()/gather | solution.py:45
  226.7 5.0 %fusion.47 = f32[4,76,224]{2,1,0:T(8,128)S(1)} fusion(bf16[4,128,28,224]{1,0,3,2:T(4,128)(2,1)} %bitcast.50, bf16[76,224,128]{2,0,1:T(8,128)(2,1)} %get-tuple-element.354, s32[]{:T(128)S(6)} %select_n.67, f32[4,76,224]{2,1,0:T(8,128)S(1)} %get-tuple-element.344, pred[]{:T(512)S(6)} %compare.11), kind=kOutput, calls=%fused_computation.19.clone.1 | convolution fusion | flops 488248320 | bytes 7540741 | tf_op jit(solution)/shard_map/while/body/eval_jaxpr/sjp,npjt->nst/dot_general | solution.py:49
  231.8 8.8 %gather_fusion.1 = bf16[28,4,128,224]{2,1,3,0:T(4,128)(2,1)} fusion(bf16[4,128,448]{1,0,2:T(4,128)(2,1)S(1)} %get-tuple-element.353, s32[28]{0:T(128)S(1)} %fusion.46), kind=kCustom, calls=%fused_computation.1.clone.clone.1 | custom fusion | bytes 12845392 | tf_op jit(solution)/shard_map/while/body/eval_jaxpr/vmap()/gather | solution.py:45
  240.6 5.0 %fusion.47 = f32[4,76,224]{2,1,0:T(8,128)S(1)} fusion(bf16[4,128,28,224]{1,0,3,2:T(4,128)(2,1)} %bitcast.50, bf16[76,224,128]{2,0,1:T(8,128)(2,1)} %get-tuple-element.354, s32[]{:T(128)S(6)} %select_n.67, f32[4,76,224]{2,1,0:T(8,128)S(1)} %get-tuple-element.344, pred[]{:T(512)S(6)} %compare.11), kind=kOutput, calls=%fused_computation.19.clone.1 | convolution fusion | flops 488248320 | bytes 7540741 | tf_op jit(solution)/shard_map/while/body/eval_jaxpr/sjp,npjt->nst/dot_general | solution.py:49
  245.7 8.8 %gather_fusion.1 = bf16[28,4,128,224]{2,1,3,0:T(4,128)(2,1)} fusion(bf16[4,128,448]{1,0,2:T(4,128)(2,1)S(1)} %get-tuple-element.353, s32[28]{0:T(128)S(1)} %fusion.46), kind=kCustom, calls=%fused_computation.1.clone.clone.1 | custom fusion | bytes 12845392 | tf_op jit(solution)/shard_map/while/body/eval_jaxpr/vmap()/gather | solution.py:45
  254.5 5.0 %fusion.47 = f32[4,76,224]{2,1,0:T(8,128)S(1)} fusion(bf16[4,128,28,224]{1,0,3,2:T(4,128)(2,1)} %bitcast.50, bf16[76,224,128]{2,0,1:T(8,128)(2,1)} %get-tuple-element.354, s32[]{:T(128)S(6)} %select_n.67, f32[4,76,224]{2,1,0:T(8,128)S(1)} %get-tuple-element.344, pred[]{:T(512)S(6)} %compare.11), kind=kOutput, calls=%fused_computation.19.clone.1 | convolution fusion | flops 488248320 | bytes 7540741 | tf_op jit(solution)/shard_map/while/body/eval_jaxpr/sjp,npjt->nst/dot_general | solution.py:49
  259.5 8.8 %gather_fusion.1 = bf16[28,4,128,224]{2,1,3,0:T(4,128)(2,1)} fusion(bf16[4,128,448]{1,0,2:T(4,128)(2,1)S(1)} %get-tuple-element.353, s32[28]{0:T(128)S(1)} %fusion.46), kind=kCustom, calls=%fused_computation.1.clone.clone.1 | custom fusion | bytes 12845392 | tf_op jit(solution)/shard_map/while/body/eval_jaxpr/vmap()/gather | solution.py:45
  268.3 5.0 %fusion.47 = f32[4,76,224]{2,1,0:T(8,128)S(1)} fusion(bf16[4,128,28,224]{1,0,3,2:T(4,128)(2,1)} %bitcast.50, bf16[76,224,128]{2,0,1:T(8,128)(2,1)} %get-tuple-element.354, s32[]{:T(128)S(6)} %select_n.67, f32[4,76,224]{2,1,0:T(8,128)S(1)} %get-tuple-element.344, pred[]{:T(512)S(6)} %compare.11), kind=kOutput, calls=%fused_computation.19.clone.1 | convolution fusion | flops 488248320 | bytes 7540741 | tf_op jit(solution)/shard_map/while/body/eval_jaxpr/sjp,npjt->nst/dot_general | solution.py:49
  273.4 8.8 %gather_fusion.1 = bf16[28,4,128,224]{2,1,3,0:T(4,128)(2,1)} fusion(bf16[4,128,448]{1,0,2:T(4,128)(2,1)S(1)} %get-tuple-element.353, s32[28]{0:T(128)S(1)} %fusion.46), kind=kCustom, calls=%fused_computation.1.clone.clone.1 | custom fusion | bytes 12845392 | tf_op jit(solution)/shard_map/while/body/eval_jaxpr/vmap()/gather | solution.py:45
  282.2 5.0 %fusion.47 = f32[4,76,224]{2,1,0:T(8,128)S(1)} fusion(bf16[4,128,28,224]{1,0,3,2:T(4,128)(2,1)} %bitcast.50, bf16[76,224,128]{2,0,1:T(8,128)(2,1)} %get-tuple-element.354, s32[]{:T(128)S(6)} %select_n.67, f32[4,76,224]{2,1,0:T(8,128)S(1)} %get-tuple-element.344, pred[]{:T(512)S(6)} %compare.11), kind=kOutput, calls=%fused_computation.19.clone.1 | convolution fusion | flops 488248320 | bytes 7540741 | tf_op jit(solution)/shard_map/while/body/eval_jaxpr/sjp,npjt->nst/dot_general | solution.py:49
  287.2 8.8 %gather_fusion.1 = bf16[28,4,128,224]{2,1,3,0:T(4,128)(2,1)} fusion(bf16[4,128,448]{1,0,2:T(4,128)(2,1)S(1)} %get-tuple-element.353, s32[28]{0:T(128)S(1)} %fusion.46), kind=kCustom, calls=%fused_computation.1.clone.clone.1 | custom fusion | bytes 12845392 | tf_op jit(solution)/shard_map/while/body/eval_jaxpr/vmap()/gather | solution.py:45
  296.0 5.0 %fusion.47 = f32[4,76,224]{2,1,0:T(8,128)S(1)} fusion(bf16[4,128,28,224]{1,0,3,2:T(4,128)(2,1)} %bitcast.50, bf16[76,224,128]{2,0,1:T(8,128)(2,1)} %get-tuple-element.354, s32[]{:T(128)S(6)} %select_n.67, f32[4,76,224]{2,1,0:T(8,128)S(1)} %get-tuple-element.344, pred[]{:T(512)S(6)} %compare.11), kind=kOutput, calls=%fused_computation.19.clone.1 | convolution fusion | flops 488248320 | bytes 7540741 | tf_op jit(solution)/shard_map/while/body/eval_jaxpr/sjp,npjt->nst/dot_general | solution.py:49
  301.1 8.8 %gather_fusion.1 = bf16[28,4,128,224]{2,1,3,0:T(4,128)(2,1)} fusion(bf16[4,128,448]{1,0,2:T(4,128)(2,1)S(1)} %get-tuple-element.353, s32[28]{0:T(128)S(1)} %fusion.46), kind=kCustom, calls=%fused_computation.1.clone.clone.1 | custom fusion | bytes 12845392 | tf_op jit(solution)/shard_map/while/body/eval_jaxpr/vmap()/gather | solution.py:45
  309.9 5.0 %fusion.47 = f32[4,76,224]{2,1,0:T(8,128)S(1)} fusion(bf16[4,128,28,224]{1,0,3,2:T(4,128)(2,1)} %bitcast.50, bf16[76,224,128]{2,0,1:T(8,128)(2,1)} %get-tuple-element.354, s32[]{:T(128)S(6)} %select_n.67, f32[4,76,224]{2,1,0:T(8,128)S(1)} %get-tuple-element.344, pred[]{:T(512)S(6)} %compare.11), kind=kOutput, calls=%fused_computation.19.clone.1 | convolution fusion | flops 488248320 | bytes 7540741 | tf_op jit(solution)/shard_map/while/body/eval_jaxpr/sjp,npjt->nst/dot_general | solution.py:49
  314.9 1.0 copy.18
  315.9 0.0 reduce-scatter.2.cloned.1.call-update
  315.9 20.6 %reduce-scatter.2.cloned.1.call-done = f32[4,76,56]{1,2,0:T(8,128)} async-done(((f32[4,76,224]{1,2,0:T(8,128)}), f32[4,76,56]{1,2,0:T(8,128)}) %reduce-scatter.2.cloned.1.call-update) | async-done | bytes 68112 | tf_op jit(solution)/shard_map/reduce_scatter | solution.py:63
  336.6 1.6 multiply_add_fusion
  (25 shorter events, 0.2 us)
Async XLA Ops:
  6.5 6.1 %copy-start = (bf16[4,76,56]{1,2,0:T(8,128)(2,1)S(1)}, bf16[4,76,56]{1,2,0:T(8,128)(2,1)}, u32[]{:S(2)}) copy-start(bf16[4,76,56]{1,2,0:T(8,128)(2,1)} %param.9) | copy-start | bytes 102148
  6.5 196.2 %all-reduce.6.cloned.1.call-start = ((), (), s32[]{:S(2)}) async-start(), calls=%async_computation.1 | async-start | bytes 917504 | tf_op jit(solution)/shard_map/psum | solution.py:60
  20.0 182.8 %copy-start.1 = (f32[128]{0:T(128)S(1)}, f32[128]{0:T(128)}, u32[]{:S(2)}) copy-start(f32[128]{0:T(128)} %param.10) | copy-start | bytes 1540
  129.0 207.6 %reduce-scatter.2.cloned.1.call-start = ((), (), s32[]{:S(2)}) async-start(), calls=%async_computation.2 | async-start | bytes 573440 | tf_op jit(solution)/shard_map/reduce_scatter | solution.py:63
  204.0 132.5 %copy-start.2 = (f32[76]{0:T(128)S(1)}, f32[76]{0:T(128)}, u32[]{:S(2)}) copy-start(f32[76]{0:T(128)} %param.11) | copy-start | bytes 916
Sparse Core Ops, SparseCore 0:
  129.1 73.6 all-reduce.5
  316.0 20.4 reduce-scatter.1
where the time goes:
time: 345 us
  local copies, waits for them, and re-layouts  149 us (43%)
  waiting for transfers between devices  94.2 us (27%)
  matrix products  77.4 us (22%)
  between operations  13.5 us (4%)
  blocking collectives  7.07 us (2%)
    psum x1, waiting for transfers between devices, on_device(): totals = lax.psum(adjoint, 'srow')  73.5 us
    gather x8, local copies, waits for them, and re-layouts, convolve_shifted(): return lax.dynamic_slice_in_dim(padded, length - first - offset, length, 2)  70.3 us
    gather x8, local copies, waits for them, and re-layouts, correlate_shifted(): return lax.dynamic_slice_in_dim(padded, first + offset, length, 2)  70.3 us
    dot_general x8, matrix products, convolve_one_turn(): jnp.einsum('sjp,npjt->nst', kernel_part, window, preferred_element_type=j...  40.2 us
    dot_general x8, matrix products, correlate_one_turn(): jnp.einsum('sjp,nsjt->npt', kernel_part, window, preferred_element_type=j...  37.2 us
    reduce_scatter x1, waiting for transfers between devices, on_device(): summed = lax.psum_scatter(forward, 'pgrp', scatter_dimension=2, tiled=True)  20.6 us
    all_gather x1, blocking collectives, on_device(): series = lax.all_gather(probes, 'pgrp', axis=2, tiled=True)  7.07 us
  transfers between devices with their start and end apart: 2, of which 2 were waited for; matrix products, arithmetic and copies ran while one was open for 0% of the time, Pallas kernels for 0%

commit v1 on v0

v1 whole, which is shorter than its diff:
```python
import functools

import jax
import jax.numpy as jnp
from jax import lax
from jax.experimental import pallas as pl
from jax.experimental.pallas import tpu as pltpu
from jax.sharding import PartitionSpec as P

LAG = 16
STEP = 2 * LAG
SENSORS = 8
F32 = jnp.float32
BF16 = jnp.bfloat16


def chunk_rows(rows, parts):
    return -(-rows // (parts * LAG)) * LAG


def start_kernel_copy(kernel_hbm, kernel_vmem, sems, piece):
    copies = []
    sensors = kernel_hbm.shape[0]
    for at, first in enumerate(range(0, sensors, piece)):
        size = min(piece, sensors - first)
        span = pl.ds(first, size)
        copy = pltpu.make_async_copy(kernel_hbm.at[span], kernel_vmem.at[span], sems.at[at])
        copy.start()
        copies.append(copy)
    return copies


def adjoint_body(
    kernel_hbm, own, from1, from2, from3, out, kernel, slices, series, lhs, total, sems, *, scale
):
    sensors, length, width = kernel.shape
    probes, part = own.shape[0], own.shape[2]
    blocks = length // STEP
    rows = probes * STEP
    piece = 2 * SENSORS
    copies = start_kernel_copy(kernel_hbm, kernel, sems, piece)
    me = lax.axis_index("pgrp")
    for offset, held in enumerate((own, from1, from2, from3)):
        slices[me ^ offset] = held[...]
    series[...] = jnp.zeros_like(series)
    for at in range(length // part):
        value = slices[at].astype(F32)
        for side in range(2):
            first = max(at * part, side * 128)
            last = min((at + 1) * part, (side + 1) * 128)
            if first < last:
                series[side, :, :sensors, first - side * 128 : last - side * 128] = value[
                    :, :, first - at * part : last - at * part
                ]
    lane = lax.broadcasted_iota(jnp.int32, (SENSORS, 128), 1)
    sub = lax.broadcasted_iota(jnp.int32, (SENSORS, 128), 0)
    groups = -(-sensors // SENSORS)
    for group in range(2 * -(-groups // 2)):
        count = max(0, min(SENSORS, sensors - group * SENSORS))
        for n in range(probes):
            low, high = [], []
            for s in range(group * SENSORS, group * SENSORS + count):
                first = series[0, n, pl.ds(s, 8, stride=0), :]
                second = series[1, n, pl.ds(s, 8, stride=0), :]
                for half in range(2):
                    shift = sub + 8 * half
                    index = (lane + shift) % 128
                    one = jnp.take_along_axis(first, index, axis=1, mode="promise_in_bounds")
                    two = jnp.take_along_axis(second, index, axis=1, mode="promise_in_bounds")
                    low.append(jnp.where(lane + shift < 128, one, two))
                    high.append(two)
            fill = [jnp.zeros((8, 128), F32)] * (2 * (SENSORS - count))
            for at, parts in enumerate((low, high)):
                turned = jnp.concatenate(parts + fill, axis=0).T.astype(BF16)
                for o in range(4 * at, min(4 * at + 4, blocks)):
                    first_row = (o - 4 * at) * STEP
                    lhs[group, o * rows + n * STEP : o * rows + (n + 1) * STEP, :] = turned[
                        first_row : first_row + STEP
                    ]
    for copy in copies:
        copy.wait()
    for j in range(blocks):
        acc = None
        for c in range(-(-sensors // piece)):
            count = min(piece, sensors - c * piece)
            span = slice(c * piece, c * piece + count)
            sides = []
            for e in range(2):
                lags = slice(STEP * j + LAG * e, STEP * j + LAG * (e + 1))
                side = kernel[span, lags, :].reshape(count * LAG, width)
                if count < piece:
                    side = jnp.concatenate(
                        [side, jnp.zeros(((piece - count) * LAG, width), BF16)], axis=0
                    )
                sides.append(side)
            right = jnp.concatenate(sides, axis=1)
            left = jnp.concatenate(
                [lhs[2 * c, j * rows :, :], lhs[2 * c + 1, j * rows :, :]], axis=1
            )
            product = jnp.dot(left, right, preferred_element_type=F32)
            acc = product if acc is None else acc + product
        span = slice(0, (blocks - j) * rows)
        if j == 0:
            total[...] = acc
        else:
            total[span, :] += acc
    if out.shape[0] > blocks * rows:
        out[blocks * rows :, :] = jnp.zeros((out.shape[0] - blocks * rows, width), F32)
    for o in range(blocks):
        for n in range(probes):
            for t in range(0, STEP, 8):
                at = o * rows + n * STEP + t
                value = total[at : at + 8, :width]
                if t < LAG:
                    value = value + total[at + LAG : at + LAG + 8, width:]
                elif o + 1 < blocks:
                    at = at + rows - LAG
                    value = value + total[at : at + 8, width:]
                out[pl.ds(o * rows + t * probes + n, 8, stride=probes), :] = value * scale


def adjoint(kernel, held, padded_rows, scale):
    sensors, length, width = kernel.shape
    probes, part = held[0].shape[0], held[0].shape[2]
    groups = 2 * -(-sensors // (2 * SENSORS))
    rows = probes * length
    return pl.pallas_call(
        functools.partial(adjoint_body, scale=scale),
        out_shape=jax.ShapeDtypeStruct((padded_rows, width), F32),
        in_specs=[pl.BlockSpec(memory_space=pl.ANY)]
        + [pl.BlockSpec(memory_space=pltpu.VMEM)] * len(held),
        out_specs=pl.BlockSpec(memory_space=pltpu.VMEM),
        scratch_shapes=[
            pltpu.VMEM(kernel.shape, BF16),
            pltpu.VMEM((length // part,) + held[0].shape, BF16),
            pltpu.VMEM((2, probes, -(-sensors // 8) * 8, 128), F32),
            pltpu.VMEM((groups, rows, 128), BF16),
            pltpu.VMEM((rows, 2 * width), F32),
            pltpu.SemaphoreType.DMA((groups // 2,)),
        ],
        name="adjoint",
    )(kernel, *held)


def merge(first, second, step, sub):
    mine = (sub & step) == 0
    return jnp.where(mine, first, second) + pltpu.roll(jnp.where(mine, second, first), step, 0)


def forward_body(
    kernel_hbm, params, own, to1, to2, to3, kernel, weights, product, held, result, sums, sems
):
    sensors, length, width = kernel.shape
    blocks = length // STEP
    rows = weights.shape[1]
    half = rows // 2
    probes = rows // STEP
    copies = start_kernel_copy(kernel_hbm, kernel, sems, 2 * SENSORS)
    for d in range(blocks):
        weights[d, :, :width] = params[d * rows : (d + 1) * rows, :]
        weights[d, half:, width:] = params[d * rows : d * rows + half, :]
        if d == 0:
            weights[d, :half, width:] = jnp.zeros((half, width), BF16)
        else:
            weights[d, :half, width:] = params[d * rows - half : d * rows, :]
    for copy in copies:
        copy.wait()
    lane = lax.broadcasted_iota(jnp.int32, (8, 128), 1)
    sub = lax.broadcasted_iota(jnp.int32, (8, 128), 0)
    sets = [(o - 1, o) for o in range(blocks - 1, 0, -2)][::-1]
    if blocks % 2:
        sets = [(0,)] + sets
    for members in sets:
        acc = None
        for j in range(members[-1] + 1):
            left = jnp.concatenate(
                [
                    kernel[:, STEP * j + LAG * e : STEP * j + LAG * (e + 1), :].reshape(
                        sensors * LAG, width
                    )
                    for e in range(2)
                ],
                axis=1,
            )
            right = jnp.concatenate(
                [
                    weights[o - j] if o >= j else jnp.zeros((rows, 2 * width), BF16)
                    for o in members
                ],
                axis=0,
            )
            part = lax.dot_general(
                left, right, (((1,), (1,)), ((), ())), preferred_element_type=F32
            )
            acc = part if acc is None else acc + part
        product[:, : len(members) * rows] = acc
        for at, o in enumerate(members):
            for group in range(-(-sensors // SENSORS)):
                summed = []
                for s in range(group * SENSORS, (group + 1) * SENSORS):
                    if s >= sensors:
                        summed.append(jnp.zeros((8, 128), F32))
                        continue
                    value = None
                    for h in range(2):
                        first = s * LAG + 8 * h
                        turned = pltpu.roll(
                            product[first : first + 8, at * rows : (at + 1) * rows],
                            8 * h * probes,
                            1,
                            stride=probes,
                            stride_axis=0,
                        )
                        inside = lane >= (sub + 8 * h) * probes
                        before = held[first : first + 8, :] if o > 0 else jnp.zeros_like(turned)
                        mixed = jnp.where(inside, turned, before)
                        if o + 1 < blocks:
                            held[first : first + 8, :] = turned
                        value = mixed if value is None else value + mixed
                    summed.append(value)
                step = 1
                while len(summed) > 1:
                    summed = [
                        merge(summed[k], summed[k + 1], step, sub)
                        for k in range(0, len(summed), 2)
                    ]
                    step *= 2
                result[group * SENSORS : (group + 1) * SENSORS, o * rows : (o + 1) * rows] = (
                    summed[0]
                )
    span = own.shape[1]
    for q in range(sums.shape[0]):
        sums[q] = result[:sensors, q * span : (q + 1) * span]
    me = lax.axis_index("pgrp")
    own[...] = sums[me]
    for offset, to in enumerate((to1, to2, to3)):
        to[...] = sums[me ^ (offset + 1)].astype(BF16)


def forward(params, kernel, probes, parts):
    sensors, length, width = kernel.shape
    rows = probes * STEP
    span = probes * length // parts
    groups = -(-sensors // (2 * SENSORS))
    padded = -(-sensors // SENSORS) * SENSORS
    return pl.pallas_call(
        forward_body,
        out_shape=[jax.ShapeDtypeStruct((sensors, span), F32)]
        + [jax.ShapeDtypeStruct((sensors, span), BF16)] * (parts - 1),
        in_specs=[
            pl.BlockSpec(memory_space=pl.ANY),
            pl.BlockSpec(memory_space=pltpu.VMEM),
        ],
        out_specs=[pl.BlockSpec(memory_space=pltpu.VMEM)] * parts,
        scratch_shapes=[
            pltpu.VMEM(kernel.shape, BF16),
            pltpu.VMEM((length // STEP, rows, 2 * width), BF16),
            pltpu.VMEM((sensors * LAG, 2 * rows), F32),
            pltpu.VMEM((sensors * LAG, rows), F32),
            pltpu.VMEM((padded, probes * length), F32),
            pltpu.VMEM((parts, sensors, span), F32),
            pltpu.SemaphoreType.DMA((groups,)),
        ],
        name="forward",
    )(kernel, params)


def finish_body(own, from1, from2, from3, probes, noise, out):
    count, sensors, part = out.shape
    total = own[...] + from1[...].astype(F32) + from2[...].astype(F32) + from3[...].astype(F32)
    span = total.shape[1]
    lane = lax.broadcasted_iota(jnp.int32, (sensors, 128), 1)
    pieces = []
    for first in range(0, span, 128):
        piece = total[:, first : first + 128]
        if piece.shape[1] < 128:
            piece = jnp.concatenate(
                [piece, jnp.zeros((sensors, 128 - piece.shape[1]), F32)], axis=1
            )
        pieces.append(piece)
    scale = jnp.broadcast_to(
        jnp.concatenate([noise[...], jnp.zeros((1, 128 - sensors), F32)], axis=1), (128, 128)
    ).T[:sensors, :]
    per = 128 // count
    for n in range(count):
        index = (count * lane + n) % 128
        value = None
        for at, piece in enumerate(pieces):
            got = jnp.take_along_axis(piece, index, axis=1, mode="promise_in_bounds")
            value = got if value is None else jnp.where(lane < at * per, value, got)
        out[n] = value[:, :part] + scale[:, :part] * probes[n].astype(F32)


def finish(own, others, probes, noise):
    count, sensors, part = probes.shape
    return pl.pallas_call(
        finish_body,
        out_shape=jax.ShapeDtypeStruct(probes.shape, F32),
        name="finish",
    )(own, *others, probes, noise.reshape(1, sensors))


def swaps(array_of, parts):
    return [
        lax.ppermute(array_of(offset), "pgrp", [(i, i ^ offset) for i in range(parts)])
        for offset in range(1, parts)
    ]


def on_device(kernel, probes, prior_var, noise_var, *, parts, peers):
    sensors, length, width = kernel.shape
    count = probes.shape[0]
    rows = count * length
    chunk = chunk_rows(rows, peers)
    held = [probes] + swaps(lambda offset: probes, parts)
    partial = adjoint(kernel, held, chunk * peers, 16.0)
    sent = partial.reshape(peers, chunk, width).astype(jnp.float16)
    got = lax.all_to_all(sent, "srow", 0, 0, tiled=True)
    totals = jnp.sum(got.astype(F32), axis=0) * (1.0 / 16.0)
    params = (totals * prior_var[None, :]).astype(BF16)
    params = jnp.broadcast_to(params[None], (peers, chunk, width))
    params = lax.all_to_all(params, "srow", 0, 0, tiled=True).reshape(peers * chunk, width)
    shares = forward(params, kernel, count, parts)
    others = swaps(lambda offset: shares[offset], parts)
    return finish(shares[0], others, probes, noise_var)


def solution(mesh):
    placed = (P("srow", None, "pgrp"), P(None, "srow", "pgrp"), P("pgrp"), P("srow"))
    body = functools.partial(
        on_device, parts=mesh.shape["pgrp"], peers=mesh.shape["srow"]
    )
    return jax.shard_map(
        body, mesh=mesh, in_specs=placed, out_specs=P(None, "srow", "pgrp"), check_vma=False
    )
```

time: 345 us -> 61.4 us (0.18)
  local copies, waits for them, and re-layouts: 149 us -> 3.91 us
  matrix products: 77.4 us -> 0 us
  waiting for transfers between devices: 94.2 us -> 16.9 us
  Pallas kernels: 0 us -> 15.7 us
  between operations: 13.5 us -> 0.08 us
  starting transfers between devices: 0.22 us -> 11.2 us
  blocking collectives: 7.07 us -> 11.4 us
    gather x16 -> x0, local copies, waits for them, and re-layouts: 141 us -> none  [the longest x8 70.3 us: convolve_shifted(): return lax.dynamic_slice_in_dim(padded, length - first - offset, length, 2)]
    dot_general x16 -> x0, matrix products: 77.4 us -> none  [the longest x8 40.2 us: convolve_one_turn(): jnp.einsum('sjp,npjt->nst', kernel_part, window, preferred_element_type=j...]
    psum x1 -> x0, waiting for transfers between devices: 73.5 us -> none  [on_device(): totals = lax.psum(adjoint, 'srow')]
    reduce_scatter x1 -> x0, waiting for transfers between devices: 20.6 us -> none  [on_device(): summed = lax.psum_scatter(forward, 'pgrp', scatter_dimension=2, tiled=True)]
    pallas_call x0 -> x3, Pallas kernels: none -> 15.7 us  [the longest x1 7.13 us: forward(): pl.pallas_call(forward_body, out_shape=[jax.ShapeDtypeStruct((sensors, sp...]
    all_to_all x0 -> x1, blocking collectives: none -> 11.4 us  [on_device(): lax.all_to_all(params, 'srow', 0, 0, tiled=True)]
    all_to_all x0 -> x1, waiting for transfers between devices: none -> 8.7 us  [on_device(): got = lax.all_to_all(sent, 'srow', 0, 0, tiled=True)]
    ppermute x0 -> x6, waiting for transfers between devices: none -> 8.16 us  [swaps(): lax.ppermute(array_of(offset), 'pgrp', [(i, i ^ offset) for i in range(pa...]
  transfers between devices with their start and end apart: 2 -> 7, of which waited for: 2 -> 5; matrix products, arithmetic and copies ran while one was open for 0% -> 0% of each run, Pallas kernels for 0% -> 0%
where the time goes in v1:
time: 61.4 us; the launch traced here: 60.9 us
  waiting for transfers between devices  16.9 us (28%)
  Pallas kernels  15.7 us (26%)
  blocking collectives  11.4 us (19%)
  starting transfers between devices  11.2 us (18%)
  local copies, waits for them, and re-layouts  3.91 us (6%)
  other arithmetic  1.79 us (3%)
    all_to_all x1, blocking collectives, on_device(): lax.all_to_all(params, 'srow', 0, 0, tiled=True)  11.4 us
    all_to_all x1, waiting for transfers between devices, on_device(): got = lax.all_to_all(sent, 'srow', 0, 0, tiled=True)  8.7 us
    ppermute x6, waiting for transfers between devices, swaps(): lax.ppermute(array_of(offset), 'pgrp', [(i, i ^ offset) for i in range(pa...  8.16 us
    pallas_call x1, Pallas kernels, forward(): pl.pallas_call(forward_body, out_shape=[jax.ShapeDtypeStruct((sensors, sp...  7.13 us
    pallas_call x1, Pallas kernels, adjoint(): pl.pallas_call(functools.partial(adjoint_body, scale=scale), out_shape=ja...  6.68 us
    all_to_all x1, starting transfers between devices, on_device(): got = lax.all_to_all(sent, 'srow', 0, 0, tiled=True)  6.04 us
    ppermute x6, starting transfers between devices, swaps(): lax.ppermute(array_of(offset), 'pgrp', [(i, i ^ offset) for i in range(pa...  5.16 us
    unnamed x17, local copies, waits for them, and re-layouts  2.21 us
  transfers between devices with their start and end apart: 7, of which 5 were waited for; matrix products, arithmetic and copies ran while one was open for 0% of the time, Pallas kernels for 0%

profile of v1, /device:TPU:0, one launch (start us, length us, event | category | flops | bytes accessed | tf_op | source)
XLA Modules:
  0.0 60.9 jit_solution(6364809581884894968)
XLA Ops:
  0.0 0.0 copy-start.7
  0.0 1.0 %copy.8.own.probes = bf16[4,76,56]{2,1,0:T(8,128)(2,1)S(1)} copy(bf16[4,76,56]{1,2,0:T(8,128)(2,1)} %param.5) | data formatting | bytes 68096 | tf_op args[1]
  1.0 0.0 copy-start
  1.0 0.6 collective-permute-start
  1.5 2.6 %collective-permute-start.1 = (bf16[4,76,56]{2,1,0:T(8,128)(2,1)S(1)}, bf16[4,76,56]{2,1,0:T(8,128)(2,1)S(1)}, u32[]{:S(2)}, u32[]{:S(2)}) collective-permute-start(bf16[4,76,56]{2,1,0:T(8,128)(2,1)S(1)} %copy.8.own.probes), channel_id=1, source_target_pairs={{0,16},{8,24},{16,0},{24,8},{1,17},{9,25},{17,1},{25,9},{2,18},{10... | collective-permute-start | bytes 102152 | tf_op jit(solution)/shard_map/ppermute | solution.py:305
  4.1 0.0 collective-permute-start.2
  4.1 0.0 collective-permute-done.from1
  4.1 0.0 copy-start.1
  4.2 3.0 %collective-permute-done.1.from2 = bf16[4,76,56]{2,1,0:T(8,128)(2,1)S(1)} collective-permute-done((bf16[4,76,56]{2,1,0:T(8,128)(2,1)S(1)}, bf16[4,76,56]{2,1,0:T(8,128)(2,1)S(1)}, u32[]{:S(2)}, u32[]{:S(2)}) %collective-permute-start.1) | collective-permute-done | bytes 34080 | tf_op jit(solution)/shard_map/ppermute | solution.py:305
  7.2 0.0 copy-start.2
  7.2 1.4 %collective-permute-done.2.from3 = bf16[4,76,56]{2,1,0:T(8,128)(2,1)S(1)} collective-permute-done((bf16[4,76,56]{2,1,0:T(8,128)(2,1)S(1)}, bf16[4,76,56]{2,1,0:T(8,128)(2,1)S(1)}, u32[]{:S(2)}, u32[]{:S(2)}) %collective-permute-start.2) | collective-permute-done | bytes 34080 | tf_op jit(solution)/shard_map/ppermute | solution.py:305
  8.6 0.0 copy-done
  8.6 0.0 copy-done.1
  8.6 0.0 copy-done.2
  8.6 0.0 copy-start.3
  8.6 0.6 %copy-done.3 = bf16[4,76,56]{2,1,0:T(8,128)(2,1)} copy-done((bf16[4,76,56]{2,1,0:T(8,128)(2,1)}, bf16[4,76,56]{2,1,0:T(8,128)(2,1)S(1)}, u32[]{:S(2)}) %copy-start.3) | copy-done | bytes 34072
  9.3 6.7 %adjoint.1 = f32[896,128]{1,0:T(8,128)} custom-call(bf16[76,224,128]{2,1,0:T(8,128)(2,1)} %kernel_hbm.3, bf16[4,76,56]{2,1,0:T(8,128)(2,1)} %copy-done, bf16[4,76,56]{2,1,0:T(8,128)(2,1)} %copy-done.1, bf16[4,76,56]{2,1,0:T(8,128)(2,1)} %copy-done.2, bf16[4,76,56]{2,1,0:T(8,128)(2,1)} %copy-done.3), custom_call_target="tpu_custom_call" | custom-call | tf_op jit(solution)/shard_map/adjoint/pallas_call | solution.py:127
  15.9 1.7 %convert_element_type.16 = f16[896,128]{1,0:T(8,128)(2,1)} convert(f32[896,128]{1,0:T(8,128)} %adjoint.1) | non-fusion elementwise | flops 114688 | bytes 688128 | tf_op jit(solution)/shard_map/convert_element_type | solution.py:317
  17.7 6.0 %all-to-all-start = ((f16[8,112,128]{2,1,0:T(8,128)(2,1)}), f16[8,112,128]{2,1,0:T(8,128)(2,1)S(1)}, u32[]{:S(2)}, u32[]{:S(2)}) async-start(f16[8,112,128]{2,1,0:T(8,128)(2,1)} %bitcast), calls=%async_computation | async-start | bytes 458752 | tf_op jit(solution)/shard_map/all_to_all | solution.py:318
  23.7 0.0 copy-done.7
  23.7 8.7 %all-to-all-done = f16[8,112,128]{2,1,0:T(8,128)(2,1)S(1)} async-done(((f16[8,112,128]{2,1,0:T(8,128)(2,1)}), f16[8,112,128]{2,1,0:T(8,128)(2,1)S(1)}, u32[]{:S(2)}, u32[]{:S(2)}) %all-to-all-start) | async-done | bytes 229408 | tf_op jit(solution)/shard_map/all_to_all | solution.py:318
  32.5 11.4 %all_to_all.10 = bf16[8,112,128]{2,1,0:T(8,128)(2,1)} all-to-all(bf16[8,112,128]{2,1,0:T(8,128)(2,1)S(1)} %broadcast_in_dim.2), channel_id=1, replica_groups=mesh['pgrp'=4,'srow'=8] {'srow'}, dimensions={0} | all-to-all | bytes 458752 | tf_op jit(solution)/shard_map/all_to_all | solution.py:322
  43.9 7.1 %forward.1 = (f32[76,224]{1,0:T(8,128)}, bf16[76,224]{1,0:T(8,128)(2,1)}, bf16[76,224]{1,0:T(8,128)(2,1)}, bf16[76,224]{1,0:T(8,128)(2,1)}) custom-call(bf16[76,224,128]{2,1,0:T(8,128)(2,1)} %kernel_hbm.3, bf16[896,128]{1,0:T(8,128)(2,1)} %bitcast.3), custom_call_target="tpu_custom_call" | custom-call | tf_op jit(solution)/shard_map/forward/pallas_call | solution.py:246
  51.1 0.1 collective-permute-start.3
  51.1 1.9 %collective-permute-start.4 = (bf16[76,224]{1,0:T(8,128)(2,1)}, bf16[76,224]{1,0:T(8,128)(2,1)S(1)}, u32[]{:S(2)}, u32[]{:S(2)}) collective-permute-start(bf16[76,224]{1,0:T(8,128)(2,1)} %get-tuple-element.11), channel_id=1, source_target_pairs={{0,16},{8,24},{16,0},{24,8},{1,17},{9,25},{17,1},{25,9},{2,18},{10... | collective-permute-start | bytes 102152 | tf_op jit(solution)/shard_map/ppermute | solution.py:305
  53.0 0.0 collective-permute-start.5
  53.1 0.0 collective-permute-done.3.from1
  53.1 0.0 copy-start.4
  53.1 2.4 %collective-permute-done.4.from2 = bf16[76,224]{1,0:T(8,128)(2,1)S(1)} collective-permute-done((bf16[76,224]{1,0:T(8,128)(2,1)}, bf16[76,224]{1,0:T(8,128)(2,1)S(1)}, u32[]{:S(2)}, u32[]{:S(2)}) %collective-permute-start.4) | collective-permute-done | bytes 34080 | tf_op jit(solution)/shard_map/ppermute | solution.py:305
  55.4 0.0 copy-start.5
  55.4 1.3 %collective-permute-done.5.from3 = bf16[76,224]{1,0:T(8,128)(2,1)S(1)} collective-permute-done((bf16[76,224]{1,0:T(8,128)(2,1)}, bf16[76,224]{1,0:T(8,128)(2,1)S(1)}, u32[]{:S(2)}, u32[]{:S(2)}) %collective-permute-start.5) | collective-permute-done | bytes 34080 | tf_op jit(solution)/shard_map/ppermute | solution.py:305
  56.8 0.0 copy-start.6
  56.8 0.0 copy-done.4
  56.8 0.0 copy-done.5
  56.8 0.6 %copy-done.6 = bf16[76,224]{1,0:T(8,128)(2,1)} copy-done((bf16[76,224]{1,0:T(8,128)(2,1)}, bf16[76,224]{1,0:T(8,128)(2,1)S(1)}, u32[]{:S(2)}) %copy-start.6) | copy-done | bytes 34072
  57.4 1.9 %finish.1 = f32[4,76,56]{2,1,0:T(8,128)} custom-call(f32[76,224]{1,0:T(8,128)} %get-tuple-element.9.own, bf16[76,224]{1,0:T(8,128)(2,1)} %copy-done.4, bf16[76,224]{1,0:T(8,128)(2,1)} %copy-done.5, bf16[76,224]{1,0:T(8,128)(2,1)} %copy-done.6, bf16[4,76,56]{2,1,0:T(8,128)(2,1)} %copy-done, f32[1,76]{1,0:T(1,128)} %bitcast.4), custom_call_target="tpu_custom_call" | custom-call | tf_op jit(solution)/shard_map/finish/pallas_call | solution.py:296
  59.2 1.7 %copy.10 = f32[4,76,56]{1,2,0:T(8,128)} copy(f32[4,76,56]{2,1,0:T(8,128)} %finish.1) | data formatting | bytes 136192 | tf_op jit(solution)/shard_map/finish/pallas_call | solution.py:296
  (4 shorter events, 0.1 us)
Async XLA Ops:
  0.0 23.7 %copy-start.7 = (f32[128]{0:T(128)S(1)}, f32[128]{0:T(128)}, u32[]{:S(2)}) copy-start(f32[128]{0:T(128)} %param.6) | copy-start | bytes 1540
  1.0 7.7 %copy-start = (bf16[4,76,56]{2,1,0:T(8,128)(2,1)}, bf16[4,76,56]{2,1,0:T(8,128)(2,1)S(1)}, u32[]{:S(2)}) copy-start(bf16[4,76,56]{2,1,0:T(8,128)(2,1)S(1)} %copy.8.own.probes) | copy-start | bytes 102148
  1.0 3.2 %collective-permute-start = (bf16[4,76,56]{2,1,0:T(8,128)(2,1)S(1)}, bf16[4,76,56]{2,1,0:T(8,128)(2,1)S(1)}, u32[]{:S(2)}, u32[]{:S(2)}) collective-permute-start(bf16[4,76,56]{2,1,0:T(8,128)(2,1)S(1)} %copy.8.own.probes), channel_id=1, source_target_pairs={{0,8},{8,0},{16,24},{24,16},{1,9},{9,1},{17,25},{25,17},{2,10},{10... | collective-permute-start | bytes 102152 | tf_op jit(solution)/shard_map/ppermute | solution.py:305
  1.5 5.7 %collective-permute-start.1 = (bf16[4,76,56]{2,1,0:T(8,128)(2,1)S(1)}, bf16[4,76,56]{2,1,0:T(8,128)(2,1)S(1)}, u32[]{:S(2)}, u32[]{:S(2)}) collective-permute-start(bf16[4,76,56]{2,1,0:T(8,128)(2,1)S(1)} %copy.8.own.probes), channel_id=1, source_target_pairs={{0,16},{8,24},{16,0},{24,8},{1,17},{9,25},{17,1},{25,9},{2,18},{10... | collective-permute-start | bytes 102152 | tf_op jit(solution)/shard_map/ppermute | solution.py:305
  4.1 4.5 %collective-permute-start.2 = (bf16[4,76,56]{2,1,0:T(8,128)(2,1)S(1)}, bf16[4,76,56]{2,1,0:T(8,128)(2,1)S(1)}, u32[]{:S(2)}, u32[]{:S(2)}) collective-permute-start(bf16[4,76,56]{2,1,0:T(8,128)(2,1)S(1)} %copy.8.own.probes), channel_id=1, source_target_pairs={{0,24},{8,16},{16,8},{24,0},{1,25},{9,17},{17,9},{25,1},{2,26},{10... | collective-permute-start | bytes 102152 | tf_op jit(solution)/shard_map/ppermute | solution.py:305
  4.1 4.5 %copy-start.1 = (bf16[4,76,56]{2,1,0:T(8,128)(2,1)}, bf16[4,76,56]{2,1,0:T(8,128)(2,1)S(1)}, u32[]{:S(2)}) copy-start(bf16[4,76,56]{2,1,0:T(8,128)(2,1)S(1)} %collective-permute-done.from1) | copy-start | bytes 102148
  7.2 1.4 %copy-start.2 = (bf16[4,76,56]{2,1,0:T(8,128)(2,1)}, bf16[4,76,56]{2,1,0:T(8,128)(2,1)S(1)}, u32[]{:S(2)}) copy-start(bf16[4,76,56]{2,1,0:T(8,128)(2,1)S(1)} %collective-permute-done.1.from2) | copy-start | bytes 102148
  8.6 0.6 %copy-start.3 = (bf16[4,76,56]{2,1,0:T(8,128)(2,1)}, bf16[4,76,56]{2,1,0:T(8,128)(2,1)S(1)}, u32[]{:S(2)}) copy-start(bf16[4,76,56]{2,1,0:T(8,128)(2,1)S(1)} %collective-permute-done.2.from3) | copy-start | bytes 102148
  17.7 14.8 %all-to-all-start = ((f16[8,112,128]{2,1,0:T(8,128)(2,1)}), f16[8,112,128]{2,1,0:T(8,128)(2,1)S(1)}, u32[]{:S(2)}, u32[]{:S(2)}) async-start(f16[8,112,128]{2,1,0:T(8,128)(2,1)} %bitcast), calls=%async_computation | async-start | bytes 458752 | tf_op jit(solution)/shard_map/all_to_all | solution.py:318
  51.1 2.0 %collective-permute-start.3 = (bf16[76,224]{1,0:T(8,128)(2,1)}, bf16[76,224]{1,0:T(8,128)(2,1)S(1)}, u32[]{:S(2)}, u32[]{:S(2)}) collective-permute-start(bf16[76,224]{1,0:T(8,128)(2,1)} %get-tuple-element.10), channel_id=1, source_target_pairs={{0,8},{8,0},{16,24},{24,16},{1,9},{9,1},{17,25},{25,17},{2,10},{10... | collective-permute-start | bytes 102152 | tf_op jit(solution)/shard_map/ppermute | solution.py:305
  51.1 4.3 %collective-permute-start.4 = (bf16[76,224]{1,0:T(8,128)(2,1)}, bf16[76,224]{1,0:T(8,128)(2,1)S(1)}, u32[]{:S(2)}, u32[]{:S(2)}) collective-permute-start(bf16[76,224]{1,0:T(8,128)(2,1)} %get-tuple-element.11), channel_id=1, source_target_pairs={{0,16},{8,24},{16,0},{24,8},{1,17},{9,25},{17,1},{25,9},{2,18},{10... | collective-permute-start | bytes 102152 | tf_op jit(solution)/shard_map/ppermute | solution.py:305
  53.0 3.7 %collective-permute-start.5 = (bf16[76,224]{1,0:T(8,128)(2,1)}, bf16[76,224]{1,0:T(8,128)(2,1)S(1)}, u32[]{:S(2)}, u32[]{:S(2)}) collective-permute-start(bf16[76,224]{1,0:T(8,128)(2,1)} %get-tuple-element.12), channel_id=1, source_target_pairs={{0,24},{8,16},{16,8},{24,0},{1,25},{9,17},{17,9},{25,1},{2,26},{10... | collective-permute-start | bytes 102152 | tf_op jit(solution)/shard_map/ppermute | solution.py:305
  53.1 3.7 %copy-start.4 = (bf16[76,224]{1,0:T(8,128)(2,1)}, bf16[76,224]{1,0:T(8,128)(2,1)S(1)}, u32[]{:S(2)}) copy-start(bf16[76,224]{1,0:T(8,128)(2,1)S(1)} %collective-permute-done.3.from1) | copy-start | bytes 102148
  55.4 1.3 %copy-start.5 = (bf16[76,224]{1,0:T(8,128)(2,1)}, bf16[76,224]{1,0:T(8,128)(2,1)S(1)}, u32[]{:S(2)}) copy-start(bf16[76,224]{1,0:T(8,128)(2,1)S(1)} %collective-permute-done.4.from2) | copy-start | bytes 102148
  56.8 0.6 %copy-start.6 = (bf16[76,224]{1,0:T(8,128)(2,1)}, bf16[76,224]{1,0:T(8,128)(2,1)S(1)}, u32[]{:S(2)}) copy-start(bf16[76,224]{1,0:T(8,128)(2,1)S(1)} %collective-permute-done.5.from3) | copy-start | bytes 102148

commit v2 on v0

v2 whole, which is shorter than its diff:
```python
import functools

import jax
import jax.numpy as jnp
from jax import lax
from jax.experimental import pallas as pl
from jax.experimental.pallas import tpu as pltpu
from jax.sharding import PartitionSpec as P

LAG = 16
STEP = 2 * LAG
SENSORS = 8
F32 = jnp.float32
BF16 = jnp.bfloat16


def in_vmem(array):
    return pltpu.with_memory_space_constraint(array, pltpu.VMEM)


def causal_sets(blocks):
    sets = [(o - 1, o) for o in range(blocks - 1, 0, -2)][::-1]
    return [(0,)] + sets if blocks % 2 else sets


def sensor_groups(sensors):
    return [
        (first, min(first + SENSORS, sensors)) for first in range(0, sensors, SENSORS)
    ]


def prepare_body(kernel_hbm, own_hbm, prior, kernel, turned, own, variance, sems):
    sensors, length, width = kernel.shape
    groups = sensor_groups(sensors)
    copies = [pltpu.make_async_copy(own_hbm, own, sems.at[len(groups)])]
    for at, (first, last) in enumerate(groups):
        span = pl.ds(first, last - first)
        copies.append(pltpu.make_async_copy(kernel_hbm.at[span], kernel.at[span], sems.at[at]))
    for copy in copies:
        copy.start()
    variance[...] = jnp.broadcast_to(prior[...], (width, width)).T
    copies[0].wait()
    for at, (first, last) in enumerate(groups):
        copies[1 + at].wait()
        for a in range(length // LAG):
            tile = kernel[first:last, a * LAG : (a + 1) * LAG, :].reshape(-1, width)
            if last - first < SENSORS:
                fill = jnp.zeros(((SENSORS - last + first) * LAG, width), BF16)
                tile = jnp.concatenate([tile, fill], axis=0)
            turned[a * width : (a + 1) * width, at * 128 : (at + 1) * 128] = tile.T
    spare = turned.shape[1] - len(groups) * 128
    if spare:
        turned[:, len(groups) * 128 :] = jnp.zeros((turned.shape[0], spare), BF16)


def prepare(kernel, series, prior_var):
    sensors, length, width = kernel.shape
    lanes = 256 * -(-sensors // (2 * SENSORS))
    vmem = pl.BlockSpec(memory_space=pltpu.VMEM)
    hbm = pl.BlockSpec(memory_space=pltpu.HBM)
    return pl.pallas_call(
        prepare_body,
        out_shape=[
            pltpu.VMEM(kernel.shape, BF16),
            pltpu.VMEM((length // LAG * width, lanes), BF16),
            pltpu.VMEM(series.shape, BF16),
            pltpu.VMEM((width, width), F32),
        ],
        in_specs=[hbm, hbm, vmem],
        out_specs=[vmem] * 4,
        scratch_shapes=[pltpu.SemaphoreType.DMA((len(sensor_groups(sensors)) + 1,))],
        compiler_params=pltpu.CompilerParams(vmem_limit_bytes=105 << 19),
        name="prepare",
    )(kernel, series, prior_var.reshape(1, width))


def adjoint_body(
    turned,
    variance,
    own,
    from1,
    from2,
    from3,
    resident,
    out,
    kept,
    tall,
    series,
    right,
    product,
    even,
    odd,
):
    width = variance.shape[0]
    probes, part, sensors = own.shape
    rows = probes * STEP
    blocks = tall.shape[0] // rows
    me = lax.axis_index("pgrp")
    for offset, held in enumerate((own, from1, from2, from3)):
        first = (me ^ offset) * (part * probes)
        for n in range(probes):
            tall[pl.ds(first + n, part, stride=probes), :sensors] = held[n].astype(F32)
    for o in range(blocks):
        series[o] = tall[o * rows : (o + 1) * rows, :].astype(BF16).T.astype(F32)
    lane = lax.broadcasted_iota(jnp.int32, (8, 128), 1)
    sub = lax.broadcasted_iota(jnp.int32, (8, 128), 0)
    sets = causal_sets(blocks)
    padded = right.shape[0] // LAG
    if padded > sensors:
        right[sensors * LAG :, :] = jnp.zeros(((padded - sensors) * LAG, right.shape[1]), BF16)

    def expand(s, first, last):
        tiles = {}
        for half in range(2):
            shift = (sub + 8 * half) * probes
            index = (lane + shift) % 128
            inside = lane + shift < 128
            held = None
            for o in range(first, min(last + 2, blocks)):
                row = series[o, pl.ds(s, 8, stride=0), :]
                moved = jnp.take_along_axis(row, index, axis=1, mode="promise_in_bounds")
                if held is not None:
                    tiles[o - 1, half] = jnp.where(inside, held, moved)
                held = moved
            if last + 1 == blocks:
                tiles[last, half] = jnp.where(inside, held, 0.0)
        for o in range(first, last + 1):
            right[s * LAG : (s + 1) * LAG, o * rows : (o + 1) * rows] = jnp.concatenate(
                [tiles[o, 0], tiles[o, 1]], axis=0
            ).astype(BF16)

    def multiply(members):
        tall_rows = (members[-1] + 1) * 2 * width
        columns = slice(members[0] * rows, (members[-1] + 1) * rows)
        pieces = -(-tall_rows // 512)
        piece = -(-tall_rows // (pieces * 128)) * 128
        for first in range(0, tall_rows, piece):
            last = min(first + piece, tall_rows)
            acc = None
            for at in range(0, turned.shape[1], 256):
                step = jnp.dot(
                    turned[first:last, at : at + 256],
                    right[at : at + 256, columns],
                    preferred_element_type=F32,
                )
                acc = step if acc is None else acc + step
            product[first:last, : len(members) * rows] = acc

    def gather(members):
        for place, o in enumerate(members):
            for j in range(o + 1):
                for e, sums in enumerate((even, odd)):
                    at = (2 * j + e) * width
                    value = product[at : at + width, place * rows : (place + 1) * rows]
                    if j == 0:
                        sums[o] = value
                    else:
                        sums[o - j] += value

    for members in sets:
        for s in range(sensors):
            expand(s, members[0], members[-1])
        multiply(members)
        gather(members)

    most = jnp.zeros((8, rows), F32)
    first_half = lane < rows // 2
    scale = variance[...]
    for first in range(0, width, 8):
        span = slice(first, first + 8)
        after = None
        for o in range(blocks - 1, -1, -1):
            moved = pltpu.roll(odd[o, span, :], rows // 2, 1)
            late = jnp.where(first_half, moved, 0.0 if after is None else after)
            after = moved
            value = (even[o, span, :] + late) * scale[span, :]
            even[o, span, :] = value
            most = jnp.maximum(most, jnp.abs(value))
    peak = jnp.maximum(jnp.max(most, axis=(0, 1), keepdims=True), 2.0**-100)
    power = jnp.floor(jnp.log2(peak))
    gain = jnp.exp2(14.0 - jnp.broadcast_to(power, (width, rows)))
    for o in range(blocks):
        out[:, o * rows : (o + 1) * rows] = even[o] * gain
    out[:, blocks * rows :] = jnp.broadcast_to(power, (width, rows))


def adjoint(turned, variance, held, resident):
    width = variance.shape[0]
    probes, part, sensors = held[0].shape
    rows = probes * STEP
    blocks = turned.shape[0] // (2 * width)
    vmem = pl.BlockSpec(memory_space=pltpu.VMEM)
    return pl.pallas_call(
        adjoint_body,
        out_shape=[
            pltpu.VMEM((width, (blocks + 1) * rows), F32),
            pltpu.VMEM(resident.shape, BF16),
        ],
        in_specs=[vmem] * (3 + len(held)),
        out_specs=[vmem, vmem],
        input_output_aliases={2 + len(held): 1},
        scratch_shapes=[
            pltpu.VMEM((blocks * rows, 128), F32),
            pltpu.VMEM((blocks, 128, rows), F32),
            pltpu.VMEM((turned.shape[1], blocks * rows), BF16),
            pltpu.VMEM((blocks * 2 * width, 2 * rows), F32),
            pltpu.VMEM((blocks, width, rows), F32),
            pltpu.VMEM((blocks, width, rows), F32),
        ],
        compiler_params=pltpu.CompilerParams(vmem_limit_bytes=24 << 20),
        name="adjoint",
    )(turned, variance, *[in_vmem(array) for array in held], resident)


def decode_body(got, out):
    peers, own_rows, columns = out.shape
    total = None
    for r in range(peers):
        gain = jnp.exp2(got[r, :, columns : columns + 128] - 14.0)
        parts = [got[r, :, at : at + 128] * gain for at in range(0, columns, 128)]
        total = parts if total is None else [x + y for x, y in zip(total, parts)]
    for at, value in enumerate(total):
        for r in range(peers):
            out[r, :, at * 128 : (at + 1) * 128] = value.astype(BF16)


def decode(got, columns):
    vmem = pl.BlockSpec(memory_space=pltpu.VMEM)
    return pl.pallas_call(
        decode_body,
        out_shape=pltpu.VMEM(got.shape[:2] + (columns,), BF16),
        in_specs=[vmem],
        out_specs=vmem,
        compiler_params=pltpu.CompilerParams(vmem_limit_bytes=24 << 20),
        name="decode",
    )(in_vmem(got))


def merge(first, second, step, sub):
    mine = (sub & step) == 0
    return jnp.where(mine, first, second) + pltpu.roll(jnp.where(mine, second, first), step, 0)


def forward_body(kernel, params, own, to1, to2, to3, weights, product, held, result, tall):
    sensors, length, width = kernel.shape
    probes, part = own.shape[0], own.shape[1]
    blocks = length // STEP
    rows = weights.shape[2]
    half = rows // 2
    for d in range(blocks):
        here = params[:, d * rows : (d + 1) * rows]
        weights[d, :width, :] = here
        if d == 0:
            before = jnp.zeros((width, half), BF16)
        else:
            before = params[:, d * rows - half : d * rows]
        weights[d, width:, :] = jnp.concatenate([before, here[:, :half]], axis=1)
    lane = lax.broadcasted_iota(jnp.int32, (8, 128), 1)
    sub = lax.broadcasted_iota(jnp.int32, (8, 128), 0)
    sets = causal_sets(blocks)

    def multiply(at, first, last):
        members = sets[at]
        acc = None
        for j in range(members[-1] + 1):
            left = jnp.concatenate(
                [
                    kernel[first:last, STEP * j + LAG * e : STEP * j + LAG * (e + 1), :].reshape(
                        (last - first) * LAG, width
                    )
                    for e in range(2)
                ],
                axis=1,
            )
            right = jnp.concatenate(
                [
                    weights[o - j] if o >= j else jnp.zeros((2 * width, rows), BF16)
                    for o in members
                ],
                axis=1,
            )
            step = jnp.dot(left, right, preferred_element_type=F32)
            acc = step if acc is None else acc + step
        product[at, first * LAG : last * LAG, : len(members) * rows] = acc

    def skew(at, group):
        for place, o in enumerate(sets[at]):
            summed = []
            for s in range(group * SENSORS, (group + 1) * SENSORS):
                if s >= sensors:
                    summed.append(jnp.zeros((8, 128), F32))
                    continue
                value = None
                for h in range(2):
                    first = s * LAG + 8 * h
                    shifted = pltpu.roll(
                        product[at, first : first + 8, place * rows : (place + 1) * rows],
                        8 * h * probes,
                        1,
                        stride=probes,
                        stride_axis=0,
                    )
                    inside = lane >= (sub + 8 * h) * probes
                    before = held[first : first + 8, :] if o > 0 else jnp.zeros_like(shifted)
                    mixed = jnp.where(inside, shifted, before)
                    if o + 1 < blocks:
                        held[first : first + 8, :] = shifted
                    value = mixed if value is None else value + mixed
                summed.append(value)
            step = 1
            while len(summed) > 1:
                summed = [
                    merge(summed[k], summed[k + 1], step, sub) for k in range(0, len(summed), 2)
                ]
                step *= 2
            result[o, group * SENSORS : (group + 1) * SENSORS, :] = summed[0]

    groups = range(-(-sensors // SENSORS))
    pieces = -(-sensors // 40)
    piece = -(-len(groups) // pieces)
    for at in range(len(sets) + 1):
        for first in range(0, len(groups), piece):
            if at < len(sets):
                multiply(at, first * SENSORS, min((first + piece) * SENSORS, sensors))
            if at > 0:
                for group in groups[first : first + piece]:
                    skew(at - 1, group)
    for o in range(blocks):
        tall[o * rows : (o + 1) * rows, :] = result[o].T
    me = lax.axis_index("pgrp")
    for offset, to in enumerate((own, to1, to2, to3)):
        first = (me ^ offset) * (part * probes)
        for n in range(probes):
            share = tall[pl.ds(first + n, part, stride=probes), :]
            to[n] = share[:, :sensors].astype(to.dtype)


def forward(params, kernel, shape, parts):
    sensors, length, width = kernel.shape
    probes = shape[0]
    rows = probes * STEP
    blocks = length // STEP
    vmem = pl.BlockSpec(memory_space=pltpu.VMEM)
    return pl.pallas_call(
        forward_body,
        out_shape=[pltpu.VMEM(shape, F32)] + [pltpu.VMEM(shape, BF16)] * (parts - 1),
        in_specs=[vmem, vmem],
        out_specs=[vmem] * parts,
        scratch_shapes=[
            pltpu.VMEM((blocks, 2 * width, rows), BF16),
            pltpu.VMEM((blocks // 2 + 1, sensors * LAG, 2 * rows), F32),
            pltpu.VMEM((sensors * LAG, rows), F32),
            pltpu.VMEM((blocks, 128, rows), F32),
            pltpu.VMEM((blocks * rows, 128), F32),
        ],
        compiler_params=pltpu.CompilerParams(vmem_limit_bytes=24 << 20),
        name="forward",
    )(kernel, in_vmem(params))


def swaps(array_of, parts):
    return [
        lax.ppermute(array_of(offset), "pgrp", [(i, i ^ offset) for i in range(parts)])
        for offset in range(1, parts)
    ]


def on_device(kernel, probes, prior_var, noise_var, *, parts, peers):
    width = kernel.shape[2]
    series = probes.transpose(0, 2, 1)
    columns = series.shape[0] * kernel.shape[1]
    others = swaps(lambda offset: series, parts)
    resident, turned, own, variance = prepare(kernel, series, prior_var)
    partial, resident = adjoint(turned, variance, [own] + others, resident)
    sent = partial.astype(jnp.float16).reshape(peers, width // peers, -1)
    got = lax.all_to_all(sent, "srow", 0, 0, tiled=True).astype(F32)
    params = decode(got, columns)
    params = lax.all_to_all(params, "srow", 0, 0, tiled=True).reshape(width, columns)
    shares = forward(params, resident, series.shape, parts)
    total = shares[0]
    for other in swaps(lambda offset: shares[offset], parts):
        total = total + other.astype(F32)
    total = total + noise_var[None, None, :] * series.astype(F32)
    return total.transpose(0, 2, 1)


def solution(mesh):
    placed = (P("srow", None, "pgrp"), P(None, "srow", "pgrp"), P("pgrp"), P("srow"))
    body = functools.partial(
        on_device, parts=mesh.shape["pgrp"], peers=mesh.shape["srow"]
    )
    return jax.shard_map(
        body, mesh=mesh, in_specs=placed, out_specs=P(None, "srow", "pgrp"), check_vma=False
    )
```

time: 345 us -> 46.8 us (0.14)
  local copies, waits for them, and re-layouts: 149 us -> 0.01 us
  waiting for transfers between devices: 94.2 us -> 4.23 us
  matrix products: 77.4 us -> 0 us
  blocking collectives: 7.07 us -> 26.1 us
  between operations: 13.5 us -> 0.09 us
  Pallas kernels: 0 us -> 10.4 us
  starting transfers between devices: 0.22 us -> 5.03 us
    gather x16 -> x0, local copies, waits for them, and re-layouts: 141 us -> none  [the longest x8 70.3 us: convolve_shifted(): return lax.dynamic_slice_in_dim(padded, length - first - offset, length, 2)]
    dot_general x16 -> x0, matrix products: 77.4 us -> none  [the longest x8 40.2 us: convolve_one_turn(): jnp.einsum('sjp,npjt->nst', kernel_part, window, preferred_element_type=j...]
    psum x1 -> x0, waiting for transfers between devices: 73.5 us -> none  [on_device(): totals = lax.psum(adjoint, 'srow')]
    all_to_all x0 -> x2, blocking collectives: none -> 26.1 us  [the longest x1 14.6 us: on_device(): got = lax.all_to_all(sent, 'srow', 0, 0, tiled=True).astype(F32)]
    reduce_scatter x1 -> x0, waiting for transfers between devices: 20.6 us -> none  [on_device(): summed = lax.psum_scatter(forward, 'pgrp', scatter_dimension=2, tiled=True)]
    pallas_call x0 -> x4, Pallas kernels: none -> 10.4 us  [the longest x1 3.61 us: adjoint(): pl.pallas_call(adjoint_body, out_shape=[pltpu.VMEM((width, (blocks + 1) *...]
    all_gather x1 -> x0, blocking collectives: 7.07 us -> none  [on_device(): series = lax.all_gather(probes, 'pgrp', axis=2, tiled=True)]
    unnamed x8 -> x4, local copies, waits for them, and re-layouts: 6.18 us -> 0.01 us
  transfers between devices with their start and end apart: 2 -> 6, of which waited for: 2 -> 3; matrix products, arithmetic and copies ran while one was open for 0% -> 0% of each run, Pallas kernels for 0% -> 8%
where the time goes in v2:
time: 46.8 us; the launch traced here: 46.6 us
  blocking collectives  26.1 us (56%)
  Pallas kernels  10.4 us (22%)
  starting transfers between devices  5.03 us (11%)
  waiting for transfers between devices  4.23 us (9%)
  other arithmetic  0.75 us (2%)
    all_to_all x1, blocking collectives, on_device(): got = lax.all_to_all(sent, 'srow', 0, 0, tiled=True).astype(F32)  14.6 us
    all_to_all x1, blocking collectives, on_device(): lax.all_to_all(params, 'srow', 0, 0, tiled=True).reshape(width, columns)  11.5 us
    ppermute x6, starting transfers between devices, swaps(): lax.ppermute(array_of(offset), 'pgrp', [(i, i ^ offset) for i in range(pa...  5.03 us
    ppermute x6, waiting for transfers between devices, swaps(): lax.ppermute(array_of(offset), 'pgrp', [(i, i ^ offset) for i in range(pa...  4.23 us
    pallas_call x1, Pallas kernels, adjoint(): pl.pallas_call(adjoint_body, out_shape=[pltpu.VMEM((width, (blocks + 1) *...  3.61 us
    pallas_call x1, Pallas kernels, prepare(): pl.pallas_call(prepare_body, out_shape=[pltpu.VMEM(kernel.shape, BF16), p...  3.55 us
    pallas_call x1, Pallas kernels, forward(): pl.pallas_call(forward_body, out_shape=[pltpu.VMEM(shape, F32)] + [pltpu....  3.17 us
  transfers between devices with their start and end apart: 6, of which 3 were waited for; matrix products, arithmetic and copies ran while one was open for 0% of the time, Pallas kernels for 8%

profile of v2, /device:TPU:0, one launch (start us, length us, event | category | flops | bytes accessed | tf_op | source)
XLA Modules:
  0.0 46.6 jit_solution(10654308637640459648)
XLA Ops:
  0.0 2.4 %collective-permute-start.2 = (bf16[4,56,76]{2,1,0:T(8,128)(2,1)}, bf16[4,56,76]{2,1,0:T(8,128)(2,1)S(1)}, u32[]{:S(2)}, u32[]{:S(2)}) collective-permute-start(bf16[4,56,76]{2,1,0:T(8,128)(2,1)} %bitcast.9), channel_id=1, source_target_pairs={{0,24},{8,16},{16,8},{24,0},{1,25},{9,17},{17,9},{25,1},{2,26},{10... | collective-permute-start | bytes 102152 | tf_op jit(solution)/shard_map/ppermute | solution.py:363
  2.4 0.6 %collective-permute-start.1 = (bf16[4,56,76]{2,1,0:T(8,128)(2,1)}, bf16[4,56,76]{2,1,0:T(8,128)(2,1)S(1)}, u32[]{:S(2)}, u32[]{:S(2)}) collective-permute-start(bf16[4,56,76]{2,1,0:T(8,128)(2,1)} %bitcast.10), channel_id=1, source_target_pairs={{0,16},{8,24},{16,0},{24,8},{1,17},{9,25},{17,1},{25,9},{2,18},{10... | collective-permute-start | bytes 102152 | tf_op jit(solution)/shard_map/ppermute | solution.py:363
  3.0 0.1 collective-permute-start
  3.1 3.5 %prepare.1 = (bf16[76,224,128]{2,1,0:T(8,128)(2,1)S(1)}, bf16[1792,1280]{1,0:T(8,128)(2,1)S(1)}, bf16[4,56,76]{2,1,0:T(8,128)(2,1)S(1)}, f32[128,128]{1,0:T(8,128)S(1)}) custom-call(bf16[76,224,128]{2,1,0:T(8,128)(2,1)} %kernel_hbm.1, bf16[4,56,76]{2,1,0:T(8,128)(2,1)} %bitcast.12, f32[1,128]{1,0:T(1,128)} %bitcast.13), custom_call_target="tpu_custom_call" | custom-call | tf_op jit(solution)/shard_map/prepare/pallas_call | solution.py:61
  6.7 0.0 collective-permute-done.2.from3
  6.7 0.5 collective-permute-done.1.from2
  7.1 0.0 collective-permute-done.from1
  7.1 3.6 %adjoint.1 = (f32[128,1024]{1,0:T(8,128)S(1)}, bf16[76,224,128]{2,1,0:T(8,128)(2,1)S(1)}) custom-call(bf16[1792,1280]{1,0:T(8,128)(2,1)S(1)} %get-tuple-element.15.turned, f32[128,128]{1,0:T(8,128)S(1)} %get-tuple-element.16.variance, bf16[4,56,76]{2,1,0:T(8,128)(2,1)S(1)} %get-tuple-element.17.own, ...), custom_call_target="tpu_custom_call", output_to_operand_aliasing={{1}: (6, {})} | custom-call | tf_op jit(solution)/shard_map/adjoint/pallas_call | solution.py:193
  10.8 0.0 copy-start
  10.8 0.0 copy-start.1
  10.8 14.6 %all_to_all.10 = f16[8,16,1024]{2,1,0:T(8,128)(2,1)S(1)} all-to-all(f16[8,16,1024]{2,1,0:T(8,128)(2,1)S(1)} %bitcast.8), channel_id=1, replica_groups=mesh['pgrp'=4,'srow'=8] {'srow'}, dimensions={0} | all-to-all | bytes 524288 | tf_op jit(solution)/shard_map/all_to_all | solution.py:376
  25.5 0.1 decode.1
  25.6 11.5 %all_to_all.11 = bf16[8,16,896]{2,1,0:T(8,128)(2,1)S(1)} all-to-all(bf16[8,16,896]{2,1,0:T(8,128)(2,1)S(1)} %decode.1), channel_id=1, replica_groups=mesh['pgrp'=4,'srow'=8] {'srow'}, dimensions={0} | all-to-all | bytes 458752 | tf_op jit(solution)/shard_map/all_to_all | solution.py:378
  37.0 3.2 %forward.1 = (f32[4,56,76]{2,1,0:T(8,128)S(1)}, bf16[4,56,76]{2,1,0:T(8,128)(2,1)S(1)}, bf16[4,56,76]{2,1,0:T(8,128)(2,1)S(1)}, bf16[4,56,76]{2,1,0:T(8,128)(2,1)S(1)}) custom-call(bf16[76,224,128]{2,1,0:T(8,128)(2,1)S(1)} %get-tuple-element.19.kernel, bf16[128,896]{1,0:T(8,128)(2,1)S(1)} %bitcast.7), custom_call_target="tpu_custom_call" | custom-call | tf_op jit(solution)/shard_map/forward/pallas_call | solution.py:344
  40.2 0.1 collective-permute-start.3
  40.3 1.7 %collective-permute-start.4 = (bf16[4,56,76]{2,1,0:T(8,128)(2,1)S(1)}, bf16[4,56,76]{2,1,0:T(8,128)(2,1)S(1)}, u32[]{:S(2)}, u32[]{:S(2)}) collective-permute-start(bf16[4,56,76]{2,1,0:T(8,128)(2,1)S(1)} %get-tuple-element.23), channel_id=1, source_target_pairs={{0,16},{8,24},{16,0},{24,8},{1,17},{9,25},{17,1},{25,9},{2,18},{10... | collective-permute-start | bytes 102152 | tf_op jit(solution)/shard_map/ppermute | solution.py:363
  42.0 0.1 collective-permute-start.5
  42.1 0.0 collective-permute-done.3
  42.1 2.5 %collective-permute-done.4 = bf16[4,56,76]{2,1,0:T(8,128)(2,1)S(1)} collective-permute-done((bf16[4,56,76]{2,1,0:T(8,128)(2,1)S(1)}, bf16[4,56,76]{2,1,0:T(8,128)(2,1)S(1)}, u32[]{:S(2)}, u32[]{:S(2)}) %collective-permute-start.4) | collective-permute-done | bytes 34080 | tf_op jit(solution)/shard_map/ppermute | solution.py:363
  44.6 1.3 %collective-permute-done.5 = bf16[4,56,76]{2,1,0:T(8,128)(2,1)S(1)} collective-permute-done((bf16[4,56,76]{2,1,0:T(8,128)(2,1)S(1)}, bf16[4,56,76]{2,1,0:T(8,128)(2,1)S(1)}, u32[]{:S(2)}, u32[]{:S(2)}) %collective-permute-start.5) | collective-permute-done | bytes 34080 | tf_op jit(solution)/shard_map/ppermute | solution.py:363
  45.9 0.0 copy-done
  45.9 0.0 copy-done.1
  45.9 0.7 %add_bitcast_fusion = f32[4,76,56]{1,2,0:T(8,128)} fusion(bf16[4,56,76]{2,1,0:T(8,128)(2,1)S(1)} %collective-permute-done.5, bf16[4,56,76]{2,1,0:T(8,128)(2,1)S(1)} %collective-permute-done.4, f32[4,56,76]{2,1,0:T(8,128)S(1)} %get-tuple-element.21, bf16[4,56,76]{2,1,0:T(8,128)(2,1)S(1)} %collective-permute-done.3, f32[76]{0:T(128)S(1)} %copy-done.1, ...), kind=kLoop, calls=%fused_computation | loop fusion | flops 153216 | bytes 272688 | tf_op jit(solution)/shard_map/transpose | solution.py:384
  (2 shorter events, 0.1 us)
Async XLA Ops:
  0.0 6.7 %collective-permute-start.2 = (bf16[4,56,76]{2,1,0:T(8,128)(2,1)}, bf16[4,56,76]{2,1,0:T(8,128)(2,1)S(1)}, u32[]{:S(2)}, u32[]{:S(2)}) collective-permute-start(bf16[4,56,76]{2,1,0:T(8,128)(2,1)} %bitcast.9), channel_id=1, source_target_pairs={{0,24},{8,16},{16,8},{24,0},{1,25},{9,17},{17,9},{25,1},{2,26},{10... | collective-permute-start | bytes 102152 | tf_op jit(solution)/shard_map/ppermute | solution.py:363
  2.4 4.7 %collective-permute-start.1 = (bf16[4,56,76]{2,1,0:T(8,128)(2,1)}, bf16[4,56,76]{2,1,0:T(8,128)(2,1)S(1)}, u32[]{:S(2)}, u32[]{:S(2)}) collective-permute-start(bf16[4,56,76]{2,1,0:T(8,128)(2,1)} %bitcast.10), channel_id=1, source_target_pairs={{0,16},{8,24},{16,0},{24,8},{1,17},{9,25},{17,1},{25,9},{2,18},{10... | collective-permute-start | bytes 102152 | tf_op jit(solution)/shard_map/ppermute | solution.py:363
  3.0 4.1 %collective-permute-start = (bf16[4,56,76]{2,1,0:T(8,128)(2,1)}, bf16[4,56,76]{2,1,0:T(8,128)(2,1)S(1)}, u32[]{:S(2)}, u32[]{:S(2)}) collective-permute-start(bf16[4,56,76]{2,1,0:T(8,128)(2,1)} %bitcast.11), channel_id=1, source_target_pairs={{0,8},{8,0},{16,24},{24,16},{1,9},{9,1},{17,25},{25,17},{2,10},{10... | collective-permute-start | bytes 102152 | tf_op jit(solution)/shard_map/ppermute | solution.py:363
  10.8 35.1 %copy-start = (bf16[4,76,56]{1,2,0:T(8,128)(2,1)S(1)}, bf16[4,76,56]{1,2,0:T(8,128)(2,1)}, u32[]{:S(2)}) copy-start(bf16[4,76,56]{1,2,0:T(8,128)(2,1)} %param.5) | copy-start | bytes 102148
  10.8 35.1 %copy-start.1 = (f32[76]{0:T(128)S(1)}, f32[76]{0:T(128)}, u32[]{:S(2)}) copy-start(f32[76]{0:T(128)} %param.7) | copy-start | bytes 916
  40.2 1.9 %collective-permute-start.3 = (bf16[4,56,76]{2,1,0:T(8,128)(2,1)S(1)}, bf16[4,56,76]{2,1,0:T(8,128)(2,1)S(1)}, u32[]{:S(2)}, u32[]{:S(2)}) collective-permute-start(bf16[4,56,76]{2,1,0:T(8,128)(2,1)S(1)} %get-tuple-element.22), channel_id=1, source_target_pairs={{0,8},{8,0},{16,24},{24,16},{1,9},{9,1},{17,25},{25,17},{2,10},{10... | collective-permute-start | bytes 102152 | tf_op jit(solution)/shard_map/ppermute | solution.py:363
  40.3 4.3 %collective-permute-start.4 = (bf16[4,56,76]{2,1,0:T(8,128)(2,1)S(1)}, bf16[4,56,76]{2,1,0:T(8,128)(2,1)S(1)}, u32[]{:S(2)}, u32[]{:S(2)}) collective-permute-start(bf16[4,56,76]{2,1,0:T(8,128)(2,1)S(1)} %get-tuple-element.23), channel_id=1, source_target_pairs={{0,16},{8,24},{16,0},{24,8},{1,17},{9,25},{17,1},{25,9},{2,18},{10... | collective-permute-start | bytes 102152 | tf_op jit(solution)/shard_map/ppermute | solution.py:363
  42.0 3.9 %collective-permute-start.5 = (bf16[4,56,76]{2,1,0:T(8,128)(2,1)S(1)}, bf16[4,56,76]{2,1,0:T(8,128)(2,1)S(1)}, u32[]{:S(2)}, u32[]{:S(2)}) collective-permute-start(bf16[4,56,76]{2,1,0:T(8,128)(2,1)S(1)} %get-tuple-element.24), channel_id=1, source_target_pairs={{0,24},{8,16},{16,8},{24,0},{1,25},{9,17},{17,9},{25,1},{2,26},{10... | collective-permute-start | bytes 102152 | tf_op jit(solution)/shard_map/ppermute | solution.py:363

commit v3 on v2

--- a/solution.py
+++ b/solution.py
@@ -10,6 +10,8 @@
 LAG = 16
 STEP = 2 * LAG
 SENSORS = 8
+NEAR = 4
+TOP = 14.0
 F32 = jnp.float32
 BF16 = jnp.bfloat16
 
@@ -74,6 +76,12 @@
     )(kernel, series, prior_var.reshape(1, width))
 
 
+def scaling(most):
+    peak = jnp.maximum(jnp.max(most, axis=(0, 1), keepdims=True), 2.0**-100)
+    power = jnp.floor(jnp.log2(peak))
+    return power, jnp.exp2(TOP - power)
+
+
 def adjoint_body(
     turned,
     variance,
@@ -82,7 +90,10 @@
     from2,
     from3,
     resident,
-    out,
+    mine,
+    to1,
+    to2,
+    to3,
     kept,
     tall,
     series,
@@ -176,12 +187,17 @@
             value = (even[o, span, :] + late) * scale[span, :]
             even[o, span, :] = value
             most = jnp.maximum(most, jnp.abs(value))
-    peak = jnp.maximum(jnp.max(most, axis=(0, 1), keepdims=True), 2.0**-100)
-    power = jnp.floor(jnp.log2(peak))
-    gain = jnp.exp2(14.0 - jnp.broadcast_to(power, (width, rows)))
+    power, gain = scaling(most)
+    block = mine.shape[0]
+    near = lax.axis_index("srow") % NEAR
     for o in range(blocks):
-        out[:, o * rows : (o + 1) * rows] = even[o] * gain
-    out[:, blocks * rows :] = jnp.broadcast_to(power, (width, rows))
+        columns = slice(o * rows, (o + 1) * rows)
+        mine[:, columns] = even[o, pl.ds(near * block, block), :]
+        for offset, to in enumerate((to1, to2, to3)):
+            first = (near ^ (offset + 1)) * block
+            to[:, columns] = even[o, pl.ds(first, block), :] * gain
+    for to in (to1, to2, to3):
+        to[:, blocks * rows :] = jnp.broadcast_to(power, (block, rows))
 
 
 def adjoint(turned, variance, held, resident):
@@ -193,12 +209,13 @@
     return pl.pallas_call(
         adjoint_body,
         out_shape=[
-            pltpu.VMEM((width, (blocks + 1) * rows), F32),
+            pltpu.VMEM((width // NEAR, blocks * rows), F32),
+            *[pltpu.VMEM((width // NEAR, (blocks + 1) * rows), F32)] * (NEAR - 1),
             pltpu.VMEM(resident.shape, BF16),
         ],
         in_specs=[vmem] * (3 + len(held)),
-        out_specs=[vmem, vmem],
-        input_output_aliases={2 + len(held): 1},
+        out_specs=[vmem] * (NEAR + 1),
+        input_output_aliases={2 + len(held): NEAR},
         scratch_shapes=[
             pltpu.VMEM((blocks * rows, 128), F32),
             pltpu.VMEM((blocks, 128, rows), F32),
@@ -212,28 +229,40 @@
     )(turned, variance, *[in_vmem(array) for array in held], resident)
 
 
-def decode_body(got, out):
-    peers, own_rows, columns = out.shape
-    total = None
-    for r in range(peers):
-        gain = jnp.exp2(got[r, :, columns : columns + 128] - 14.0)
-        parts = [got[r, :, at : at + 128] * gain for at in range(0, columns, 128)]
-        total = parts if total is None else [x + y for x, y in zip(total, parts)]
-    for at, value in enumerate(total):
-        for r in range(peers):
-            out[r, :, at * 128 : (at + 1) * 128] = value.astype(BF16)
-
-
-def decode(got, columns):
+def combine_body(mine, *refs, count, final):
+    got, outs = refs[:count], refs[count:]
+    block, columns = mine.shape
+    gains = [jnp.exp2(ref[:, columns:] - TOP) for ref in got]
+    most = jnp.zeros((8, 128), F32)
+    for at in range(0, columns, 128):
+        span = slice(at, at + 128)
+        total = mine[:, span]
+        for ref, gain in zip(got, gains):
+            total = total + ref[:, span] * gain
+        outs[0][:, span] = total.astype(outs[0].dtype)
+        if not final:
+            for first in range(0, block, 8):
+                most = jnp.maximum(most, jnp.abs(total[first : first + 8]))
+    if not final:
+        power, gain = scaling(most)
+        outs[1][:, :columns] = outs[0][...] * gain
+        outs[1][:, columns:] = jnp.broadcast_to(power, (block, 128))
+
+
+def combine(mine, got, final):
     vmem = pl.BlockSpec(memory_space=pltpu.VMEM)
+    if final:
+        outs = [pltpu.VMEM(mine.shape, BF16)]
+    else:
+        outs = [pltpu.VMEM(mine.shape, F32), pltpu.VMEM(got[0].shape, F32)]
     return pl.pallas_call(
-        decode_body,
-        out_shape=pltpu.VMEM(got.shape[:2] + (columns,), BF16),
-        in_specs=[vmem],
-        out_specs=vmem,
+        functools.partial(combine_body, count=len(got), final=final),
+        out_shape=outs,
+        in_specs=[vmem] * (1 + len(got)),
+        out_specs=[vmem] * len(outs),
         compiler_params=pltpu.CompilerParams(vmem_limit_bytes=24 << 20),
-        name="decode",
-    )(in_vmem(got))
+        name="combine",
+    )(mine, *[in_vmem(array) for array in got])
 
 
 def merge(first, second, step, sub):
@@ -241,12 +270,31 @@
     return jnp.where(mine, first, second) + pltpu.roll(jnp.where(mine, second, first), step, 0)
 
 
-def forward_body(kernel, params, own, to1, to2, to3, weights, product, held, result, tall):
+def forward_body(
+    kernel,
+    params0,
+    params1,
+    params2,
+    params3,
+    own,
+    across,
+    beside,
+    params,
+    weights,
+    product,
+    held,
+    result,
+    tall,
+):
     sensors, length, width = kernel.shape
     probes, part = own.shape[0], own.shape[1]
     blocks = length // STEP
     rows = weights.shape[2]
     half = rows // 2
+    block = params0.shape[0]
+    near = lax.axis_index("srow") % NEAR
+    for offset, piece in enumerate((params0, params1, params2, params3)):
+        params[pl.ds(pl.multiple_of((near ^ offset) * block, block), block), :] = piece[...]
     for d in range(blocks):
         here = params[:, d * rows : (d + 1) * rows]
         weights[d, :width, :] = here
@@ -328,14 +376,14 @@
     for o in range(blocks):
         tall[o * rows : (o + 1) * rows, :] = result[o].T
     me = lax.axis_index("pgrp")
-    for offset, to in enumerate((own, to1, to2, to3)):
+    for offset, to in ((0, own), (2, across), (1, beside.at[0]), (3, beside.at[1])):
         first = (me ^ offset) * (part * probes)
         for n in range(probes):
             share = tall[pl.ds(first + n, part, stride=probes), :]
             to[n] = share[:, :sensors].astype(to.dtype)
 
 
-def forward(params, kernel, shape, parts):
+def forward(params, kernel, shape):
     sensors, length, width = kernel.shape
     probes = shape[0]
     rows = probes * STEP
@@ -343,10 +391,15 @@
     vmem = pl.BlockSpec(memory_space=pltpu.VMEM)
     return pl.pallas_call(
         forward_body,
-        out_shape=[pltpu.VMEM(shape, F32)] + [pltpu.VMEM(shape, BF16)] * (parts - 1),
-        in_specs=[vmem, vmem],
-        out_specs=[vmem] * parts,
+        out_shape=[
+            pltpu.VMEM(shape, F32),
+            pltpu.VMEM(shape, F32),
+            pltpu.VMEM((2,) + shape, BF16),
+        ],
+        in_specs=[vmem] * (1 + NEAR),
+        out_specs=[vmem] * 3,
         scratch_shapes=[
+            pltpu.VMEM((width, blocks * rows), BF16),
             pltpu.VMEM((blocks, 2 * width, rows), BF16),
             pltpu.VMEM((blocks // 2 + 1, sensors * LAG, 2 * rows), F32),
             pltpu.VMEM((sensors * LAG, rows), F32),
@@ -355,40 +408,44 @@
         ],
         compiler_params=pltpu.CompilerParams(vmem_limit_bytes=24 << 20),
         name="forward",
-    )(kernel, in_vmem(params))
-
-
-def swaps(array_of, parts):
-    return [
-        lax.ppermute(array_of(offset), "pgrp", [(i, i ^ offset) for i in range(parts)])
-        for offset in range(1, parts)
-    ]
+    )(kernel, *[in_vmem(array) for array in params])
+
+
+def swap(array, axis, size, offset):
+    return lax.ppermute(array, axis, [(i, i ^ offset) for i in range(size)])
+
+
+def swap_sums(array, size, offset):
+    return swap(array.astype(jnp.float16), "srow", size, offset).astype(F32)
 
 
 def on_device(kernel, probes, prior_var, noise_var, *, parts, peers):
-    width = kernel.shape[2]
     series = probes.transpose(0, 2, 1)
-    columns = series.shape[0] * kernel.shape[1]
-    others = swaps(lambda offset: series, parts)
+    others = [swap(series, "pgrp", parts, offset) for offset in range(1, parts)]
     resident, turned, own, variance = prepare(kernel, series, prior_var)
-    partial, resident = adjoint(turned, variance, [own] + others, resident)
-    sent = partial.astype(jnp.float16).reshape(peers, width // peers, -1)
-    got = lax.all_to_all(sent, "srow", 0, 0, tiled=True).astype(F32)
-    params = decode(got, columns)
-    params = lax.all_to_all(params, "srow", 0, 0, tiled=True).reshape(width, columns)
-    shares = forward(params, resident, series.shape, parts)
-    total = shares[0]
-    for other in swaps(lambda offset: shares[offset], parts):
-        total = total + other.astype(F32)
+    mine, *sent, resident = adjoint(turned, variance, [own] + others, resident)
+    got = [swap_sums(sent[offset - 1], peers, offset) for offset in range(1, NEAR)]
+    offset = NEAR
+    while offset < peers:
+        mine, away = combine(mine, got, False)
+        got = [swap_sums(away, peers, offset)]
+        offset *= 2
+    (params,) = combine(mine, got, True)
+    params = [params] + [swap(params, "srow", peers, offset) for offset in range(1, NEAR)]
+    own, across, beside = forward(params, resident, series.shape)
+    beside = swap(beside, "pgrp", parts, 1).astype(F32)
+    across = swap((across + beside[1]).astype(BF16), "pgrp", parts, 2)
+    total = own + beside[0] + across.astype(F32)
     total = total + noise_var[None, None, :] * series.astype(F32)
     return total.transpose(0, 2, 1)
 
 
 def solution(mesh):
     placed = (P("srow", None, "pgrp"), P(None, "srow", "pgrp"), P("pgrp"), P("srow"))
-    body = functools.partial(
-        on_device, parts=mesh.shape["pgrp"], peers=mesh.shape["srow"]
-    )
+    parts, peers = mesh.shape["pgrp"], mesh.shape["srow"]
+    if parts != 4 or peers < NEAR or peers & (peers - 1):
+        raise ValueError("unsupported mesh")
+    body = functools.partial(on_device, parts=parts, peers=peers)
     return jax.shard_map(
         body, mesh=mesh, in_specs=placed, out_specs=P(None, "srow", "pgrp"), check_vma=False
     )

time: 46.8 us -> 39.6 us (0.85)
  blocking collectives: 26.1 us -> 0 us
  starting transfers between devices: 5.03 us -> 14.7 us
  waiting for transfers between devices: 4.23 us -> 13.3 us
    all_to_all x2 -> x0, blocking collectives: 26.1 us -> none  [the longest x1 14.6 us: on_device(): got = lax.all_to_all(sent, 'srow', 0, 0, tiled=True).astype(F32)]
    ppermute x6 -> x12, starting transfers between devices: 5.03 us -> 14.7 us  [swap(): return lax.ppermute(array, axis, [(i, i ^ offset) for i in range(size)])]
    ppermute x6 -> x12, waiting for transfers between devices: 4.23 us -> 13.3 us  [swap(): return lax.ppermute(array, axis, [(i, i ^ offset) for i in range(size)])]
    pallas_call x3 -> x4, Pallas kernels: 6.83 us -> 6.98 us  [the longest x1 3.59 us: adjoint(): pl.pallas_call(adjoint_body, out_shape=[pltpu.VMEM((width // NEAR, blocks...]
  transfers between devices with their start and end apart: 6 -> 12, of which waited for: 3 -> 10; matrix products, arithmetic and copies ran while one was open for 0% -> 0% of each run, Pallas kernels for 8% -> 9%
where the time goes in v3:
time: 39.6 us; the launch traced here: 39.5 us
  starting transfers between devices  14.7 us (37%)
  waiting for transfers between devices  13.3 us (34%)
  Pallas kernels  10.5 us (27%)
  other arithmetic  0.8 us (2%)
    ppermute x12, starting transfers between devices, swap(): return lax.ppermute(array, axis, [(i, i ^ offset) for i in range(size)])  14.7 us
    ppermute x12, waiting for transfers between devices, swap(): return lax.ppermute(array, axis, [(i, i ^ offset) for i in range(size)])  13.3 us
    pallas_call x1, Pallas kernels, adjoint(): pl.pallas_call(adjoint_body, out_shape=[pltpu.VMEM((width // NEAR, blocks...  3.59 us
    pallas_call x1, Pallas kernels, prepare(): pl.pallas_call(prepare_body, out_shape=[pltpu.VMEM(kernel.shape, BF16), p...  3.55 us
    pallas_call x1, Pallas kernels, forward(): pl.pallas_call(forward_body, out_shape=[pltpu.VMEM(shape, F32), pltpu.VME...  3.19 us
  transfers between devices with their start and end apart: 12, of which 10 were waited for; matrix products, arithmetic and copies ran while one was open for 0% of the time, Pallas kernels for 9%

profile of v3, /device:TPU:0, one launch (start us, length us, event | category | flops | bytes accessed | tf_op | source)
XLA Modules:
  0.0 39.5 jit_solution(3966500019122310657)
XLA Ops:
  0.0 2.4 %collective-permute-start.2 = (bf16[4,56,76]{2,1,0:T(8,128)(2,1)}, bf16[4,56,76]{2,1,0:T(8,128)(2,1)S(1)}, u32[]{:S(2)}, u32[]{:S(2)}) collective-permute-start(bf16[4,56,76]{2,1,0:T(8,128)(2,1)} %bitcast.21), channel_id=1, source_target_pairs={{0,24},{8,16},{16,8},{24,0},{1,25},{9,17},{17,9},{25,1},{2,26},{10... | collective-permute-start | bytes 102152 | tf_op jit(solution)/shard_map/ppermute | solution.py:415
  2.4 0.6 %collective-permute-start.1 = (bf16[4,56,76]{2,1,0:T(8,128)(2,1)}, bf16[4,56,76]{2,1,0:T(8,128)(2,1)S(1)}, u32[]{:S(2)}, u32[]{:S(2)}) collective-permute-start(bf16[4,56,76]{2,1,0:T(8,128)(2,1)} %bitcast.22), channel_id=1, source_target_pairs={{0,16},{8,24},{16,0},{24,8},{1,17},{9,25},{17,1},{25,9},{2,18},{10... | collective-permute-start | bytes 102152 | tf_op jit(solution)/shard_map/ppermute | solution.py:415
  3.0 0.1 collective-permute-start
  3.1 3.5 %prepare.1 = (bf16[76,224,128]{2,1,0:T(8,128)(2,1)S(1)}, bf16[1792,1280]{1,0:T(8,128)(2,1)S(1)}, bf16[4,56,76]{2,1,0:T(8,128)(2,1)S(1)}, f32[128,128]{1,0:T(8,128)S(1)}) custom-call(bf16[76,224,128]{2,1,0:T(8,128)(2,1)} %kernel_hbm.1, bf16[4,56,76]{2,1,0:T(8,128)(2,1)} %bitcast.24, f32[1,128]{1,0:T(1,128)} %bitcast.25), custom_call_target="tpu_custom_call" | custom-call | tf_op jit(solution)/shard_map/prepare/pallas_call | solution.py:63
  6.7 0.0 collective-permute-done.2.from3
  6.7 0.5 %collective-permute-done.1.from2 = bf16[4,56,76]{2,1,0:T(8,128)(2,1)S(1)} collective-permute-done((bf16[4,56,76]{2,1,0:T(8,128)(2,1)}, bf16[4,56,76]{2,1,0:T(8,128)(2,1)S(1)}, u32[]{:S(2)}, u32[]{:S(2)}) %collective-permute-start.1) | collective-permute-done | bytes 34080 | tf_op jit(solution)/shard_map/ppermute | solution.py:415
  7.1 0.0 collective-permute-done.from1
  7.1 3.6 %adjoint.1 = (f32[32,896]{1,0:T(8,128)S(1)}, f32[32,1024]{1,0:T(8,128)S(1)}, f32[32,1024]{1,0:T(8,128)S(1)}, f32[32,1024]{1,0:T(8,128)S(1)}, bf16[76,224,128]{2,1,0:T(8,128)(2,1)S(1)}) custom-call(bf16[1792,1280]{1,0:T(8,128)(2,1)S(1)} %get-tuple-element.19.turned, f32[128,128]{1,0:T(8,128)S(1)} %get-tuple-element.20.variance, ...), custom_call_target="tpu_custom_call", output_to_operand_aliasing={{4}: (6, {})} | custom-call | tf_op jit(solution)/shard_map/adjoint/pallas_call | solution.py:209
  10.7 0.0 copy-start
  10.8 0.0 copy-start.1
  10.8 2.6 %collective-permute-start.5 = (f16[32,1024]{1,0:T(8,128)(2,1)S(1)}, f16[32,1024]{1,0:T(8,128)(2,1)S(1)}, u32[]{:S(2)}, u32[]{:S(2)}) collective-permute-start(f16[32,1024]{1,0:T(8,128)(2,1)S(1)} %convert_element_type.40), channel_id=1, source_target_pairs={{0,3},{1,2},{2,1},{3,0},{4,7},{5,6},{6,5},{7,4},{8,11},{9,10},{10,... | collective-permute-start | bytes 196616 | tf_op jit(solution)/shard_map/ppermute | solution.py:415
  13.4 0.4 %collective-permute-start.4 = (f16[32,1024]{1,0:T(8,128)(2,1)S(1)}, f16[32,1024]{1,0:T(8,128)(2,1)S(1)}, u32[]{:S(2)}, u32[]{:S(2)}) collective-permute-start(f16[32,1024]{1,0:T(8,128)(2,1)S(1)} %convert_element_type.38), channel_id=1, source_target_pairs={{0,2},{1,3},{2,0},{3,1},{4,6},{5,7},{6,4},{7,5},{8,10},{9,11},{10,... | collective-permute-start | bytes 196616 | tf_op jit(solution)/shard_map/ppermute | solution.py:415
  13.8 0.6 %collective-permute-start.3 = (f16[32,1024]{1,0:T(8,128)(2,1)S(1)}, f16[32,1024]{1,0:T(8,128)(2,1)S(1)}, u32[]{:S(2)}, u32[]{:S(2)}) collective-permute-start(f16[32,1024]{1,0:T(8,128)(2,1)S(1)} %convert_element_type.36), channel_id=1, source_target_pairs={{0,1},{1,0},{2,3},{3,2},{4,5},{5,4},{6,7},{7,6},{8,9},{9,8},{10,11... | collective-permute-start | bytes 196616 | tf_op jit(solution)/shard_map/ppermute | solution.py:415
  14.4 2.0 %collective-permute-done.5 = f16[32,1024]{1,0:T(8,128)(2,1)S(1)} collective-permute-done((f16[32,1024]{1,0:T(8,128)(2,1)S(1)}, f16[32,1024]{1,0:T(8,128)(2,1)S(1)}, u32[]{:S(2)}, u32[]{:S(2)}) %collective-permute-start.5) | collective-permute-done | bytes 65568 | tf_op jit(solution)/shard_map/ppermute | solution.py:415
  16.5 1.2 %collective-permute-done.4 = f16[32,1024]{1,0:T(8,128)(2,1)S(1)} collective-permute-done((f16[32,1024]{1,0:T(8,128)(2,1)S(1)}, f16[32,1024]{1,0:T(8,128)(2,1)S(1)}, u32[]{:S(2)}, u32[]{:S(2)}) %collective-permute-start.4) | collective-permute-done | bytes 65568 | tf_op jit(solution)/shard_map/ppermute | solution.py:415
  17.7 0.5 %collective-permute-done.3 = f16[32,1024]{1,0:T(8,128)(2,1)S(1)} collective-permute-done((f16[32,1024]{1,0:T(8,128)(2,1)S(1)}, f16[32,1024]{1,0:T(8,128)(2,1)S(1)}, u32[]{:S(2)}, u32[]{:S(2)}) %collective-permute-start.3) | collective-permute-done | bytes 65568 | tf_op jit(solution)/shard_map/ppermute | solution.py:415
  18.2 0.2 combine.2
  18.4 2.7 %collective-permute-start.6 = (f16[32,1024]{1,0:T(8,128)(2,1)S(1)}, f16[32,1024]{1,0:T(8,128)(2,1)S(1)}, u32[]{:S(2)}, u32[]{:S(2)}) collective-permute-start(f16[32,1024]{1,0:T(8,128)(2,1)S(1)} %convert_element_type.42), channel_id=1, source_target_pairs={{0,4},{1,5},{2,6},{3,7},{4,0},{5,1},{6,2},{7,3},{8,12},{9,13},{10,... | collective-permute-start | bytes 196616 | tf_op jit(solution)/shard_map/ppermute | solution.py:415
  21.0 2.6 %collective-permute-done.6 = f16[32,1024]{1,0:T(8,128)(2,1)S(1)} collective-permute-done((f16[32,1024]{1,0:T(8,128)(2,1)S(1)}, f16[32,1024]{1,0:T(8,128)(2,1)S(1)}, u32[]{:S(2)}, u32[]{:S(2)}) %collective-permute-start.6) | collective-permute-done | bytes 65568 | tf_op jit(solution)/shard_map/ppermute | solution.py:415
  23.7 1.6 %collective-permute-start.9 = (bf16[32,896]{1,0:T(8,128)(2,1)S(1)}, bf16[32,896]{1,0:T(8,128)(2,1)S(1)}, u32[]{:S(2)}, u32[]{:S(2)}) collective-permute-start(bf16[32,896]{1,0:T(8,128)(2,1)S(1)} %combine.3.params0), channel_id=1, source_target_pairs={{0,3},{1,2},{2,1},{3,0},{4,7},{5,6},{6,5},{7,4},{8,11},{9,10},{10,... | collective-permute-start | bytes 172040 | tf_op jit(solution)/shard_map/ppermute | solution.py:415
  25.3 0.5 %collective-permute-start.8 = (bf16[32,896]{1,0:T(8,128)(2,1)S(1)}, bf16[32,896]{1,0:T(8,128)(2,1)S(1)}, u32[]{:S(2)}, u32[]{:S(2)}) collective-permute-start(bf16[32,896]{1,0:T(8,128)(2,1)S(1)} %combine.3.params0), channel_id=1, source_target_pairs={{0,2},{1,3},{2,0},{3,1},{4,6},{5,7},{6,4},{7,5},{8,10},{9,11},{10,... | collective-permute-start | bytes 172040 | tf_op jit(solution)/shard_map/ppermute | solution.py:415
  25.7 1.5 %collective-permute-start.7 = (bf16[32,896]{1,0:T(8,128)(2,1)S(1)}, bf16[32,896]{1,0:T(8,128)(2,1)S(1)}, u32[]{:S(2)}, u32[]{:S(2)}) collective-permute-start(bf16[32,896]{1,0:T(8,128)(2,1)S(1)} %combine.3.params0), channel_id=1, source_target_pairs={{0,1},{1,0},{2,3},{3,2},{4,5},{5,4},{6,7},{7,6},{8,9},{9,8},{10,11... | collective-permute-start | bytes 172040 | tf_op jit(solution)/shard_map/ppermute | solution.py:415
  27.2 1.6 %collective-permute-done.9.params3 = bf16[32,896]{1,0:T(8,128)(2,1)S(1)} collective-permute-done((bf16[32,896]{1,0:T(8,128)(2,1)S(1)}, bf16[32,896]{1,0:T(8,128)(2,1)S(1)}, u32[]{:S(2)}, u32[]{:S(2)}) %collective-permute-start.9) | collective-permute-done | bytes 57376 | tf_op jit(solution)/shard_map/ppermute | solution.py:415
  28.8 0.7 %collective-permute-done.8.params2 = bf16[32,896]{1,0:T(8,128)(2,1)S(1)} collective-permute-done((bf16[32,896]{1,0:T(8,128)(2,1)S(1)}, bf16[32,896]{1,0:T(8,128)(2,1)S(1)}, u32[]{:S(2)}, u32[]{:S(2)}) %collective-permute-start.8) | collective-permute-done | bytes 57376 | tf_op jit(solution)/shard_map/ppermute | solution.py:415
  29.5 0.5 %collective-permute-done.7.params1 = bf16[32,896]{1,0:T(8,128)(2,1)S(1)} collective-permute-done((bf16[32,896]{1,0:T(8,128)(2,1)S(1)}, bf16[32,896]{1,0:T(8,128)(2,1)S(1)}, u32[]{:S(2)}, u32[]{:S(2)}) %collective-permute-start.7) | collective-permute-done | bytes 57376 | tf_op jit(solution)/shard_map/ppermute | solution.py:415
  29.9 3.2 %forward.1 = (f32[4,56,76]{2,1,0:T(8,128)S(1)}, f32[4,56,76]{2,1,0:T(8,128)S(1)}, bf16[2,4,56,76]{3,2,1,0:T(8,128)(2,1)S(1)}) custom-call(bf16[76,224,128]{2,1,0:T(8,128)(2,1)S(1)} %get-tuple-element.23.kernel, bf16[32,896]{1,0:T(8,128)(2,1)S(1)} %combine.3.params0, bf16[32,896]{1,0:T(8,128)(2,1)S(1)} %collective-permute-done.7.params1, ...), custom_call_target="tpu_custom_call" | custom-call | tf_op jit(solution)/shard_map/forward/pallas_call | solution.py:392
  33.1 0.1 collective-permute-start.10
  33.2 1.3 %collective-permute-done.10 = bf16[2,4,56,76]{3,2,1,0:T(8,128)(2,1)S(1)} collective-permute-done((bf16[2,4,56,76]{3,2,1,0:T(8,128)(2,1)S(1)}, bf16[2,4,56,76]{3,2,1,0:T(8,128)(2,1)S(1)}, u32[]{:S(2)}, u32[]{:S(2)}) %collective-permute-start.10) | collective-permute-done | bytes 68128 | tf_op jit(solution)/shard_map/ppermute | solution.py:415
  34.5 1.6 %collective-permute-start.11 = (bf16[4,56,76]{2,1,0:T(8,128)(2,1)S(1)}, bf16[4,56,76]{2,1,0:T(8,128)(2,1)S(1)}, u32[]{:S(2)}, u32[]{:S(2)}) collective-permute-start(bf16[4,56,76]{2,1,0:T(8,128)(2,1)S(1)} %fusion.1), channel_id=1, source_target_pairs={{0,16},{8,24},{16,0},{24,8},{1,17},{9,25},{17,1},{25,9},{2,18},{10... | collective-permute-start | bytes 102152 | tf_op jit(solution)/shard_map/ppermute | solution.py:415
  36.2 2.6 %collective-permute-done.11 = bf16[4,56,76]{2,1,0:T(8,128)(2,1)S(1)} collective-permute-done((bf16[4,56,76]{2,1,0:T(8,128)(2,1)S(1)}, bf16[4,56,76]{2,1,0:T(8,128)(2,1)S(1)}, u32[]{:S(2)}, u32[]{:S(2)}) %collective-permute-start.11) | collective-permute-done | bytes 34080 | tf_op jit(solution)/shard_map/ppermute | solution.py:415
  38.8 0.0 copy-done
  38.8 0.0 copy-done.1
  38.8 0.7 %fusion.5 = f32[4,76,56]{1,2,0:T(8,128)} fusion(f32[4,56,76]{2,1,0:T(8,128)S(1)} %get-tuple-element.30, f32[2,4,56,76]{3,2,1,0:T(8,128)S(1)} %convert_element_type.44, bf16[4,56,76]{2,1,0:T(8,128)(2,1)S(1)} %collective-permute-done.11, f32[76]{0:T(128)S(1)} %copy-done.1, bf16[4,76,56]{1,2,0:T(8,128)(2,1)S(1)} %copy-done), kind=kLoop, calls=%fused_computation.7 | loop fusion | flops 102144 | bytes 272688 | tf_op jit(solution)/shard_map/transpose | solution.py:440
  (11 shorter events, 0.1 us)
Async XLA Ops:
  0.0 6.7 %collective-permute-start.2 = (bf16[4,56,76]{2,1,0:T(8,128)(2,1)}, bf16[4,56,76]{2,1,0:T(8,128)(2,1)S(1)}, u32[]{:S(2)}, u32[]{:S(2)}) collective-permute-start(bf16[4,56,76]{2,1,0:T(8,128)(2,1)} %bitcast.21), channel_id=1, source_target_pairs={{0,24},{8,16},{16,8},{24,0},{1,25},{9,17},{17,9},{25,1},{2,26},{10... | collective-permute-start | bytes 102152 | tf_op jit(solution)/shard_map/ppermute | solution.py:415
  2.4 4.7 %collective-permute-start.1 = (bf16[4,56,76]{2,1,0:T(8,128)(2,1)}, bf16[4,56,76]{2,1,0:T(8,128)(2,1)S(1)}, u32[]{:S(2)}, u32[]{:S(2)}) collective-permute-start(bf16[4,56,76]{2,1,0:T(8,128)(2,1)} %bitcast.22), channel_id=1, source_target_pairs={{0,16},{8,24},{16,0},{24,8},{1,17},{9,25},{17,1},{25,9},{2,18},{10... | collective-permute-start | bytes 102152 | tf_op jit(solution)/shard_map/ppermute | solution.py:415
  3.0 4.1 %collective-permute-start = (bf16[4,56,76]{2,1,0:T(8,128)(2,1)}, bf16[4,56,76]{2,1,0:T(8,128)(2,1)S(1)}, u32[]{:S(2)}, u32[]{:S(2)}) collective-permute-start(bf16[4,56,76]{2,1,0:T(8,128)(2,1)} %bitcast.23), channel_id=1, source_target_pairs={{0,8},{8,0},{16,24},{24,16},{1,9},{9,1},{17,25},{25,17},{2,10},{10... | collective-permute-start | bytes 102152 | tf_op jit(solution)/shard_map/ppermute | solution.py:415
  10.7 28.0 %copy-start = (bf16[4,76,56]{1,2,0:T(8,128)(2,1)S(1)}, bf16[4,76,56]{1,2,0:T(8,128)(2,1)}, u32[]{:S(2)}) copy-start(bf16[4,76,56]{1,2,0:T(8,128)(2,1)} %param.5) | copy-start | bytes 102148
  10.8 28.0 %copy-start.1 = (f32[76]{0:T(128)S(1)}, f32[76]{0:T(128)}, u32[]{:S(2)}) copy-start(f32[76]{0:T(128)} %param.7) | copy-start | bytes 916
  10.8 5.6 %collective-permute-start.5 = (f16[32,1024]{1,0:T(8,128)(2,1)S(1)}, f16[32,1024]{1,0:T(8,128)(2,1)S(1)}, u32[]{:S(2)}, u32[]{:S(2)}) collective-permute-start(f16[32,1024]{1,0:T(8,128)(2,1)S(1)} %convert_element_type.40), channel_id=1, source_target_pairs={{0,3},{1,2},{2,1},{3,0},{4,7},{5,6},{6,5},{7,4},{8,11},{9,10},{10,... | collective-permute-start | bytes 196616 | tf_op jit(solution)/shard_map/ppermute | solution.py:415
  13.4 4.3 %collective-permute-start.4 = (f16[32,1024]{1,0:T(8,128)(2,1)S(1)}, f16[32,1024]{1,0:T(8,128)(2,1)S(1)}, u32[]{:S(2)}, u32[]{:S(2)}) collective-permute-start(f16[32,1024]{1,0:T(8,128)(2,1)S(1)} %convert_element_type.38), channel_id=1, source_target_pairs={{0,2},{1,3},{2,0},{3,1},{4,6},{5,7},{6,4},{7,5},{8,10},{9,11},{10,... | collective-permute-start | bytes 196616 | tf_op jit(solution)/shard_map/ppermute | solution.py:415
  13.8 4.3 %collective-permute-start.3 = (f16[32,1024]{1,0:T(8,128)(2,1)S(1)}, f16[32,1024]{1,0:T(8,128)(2,1)S(1)}, u32[]{:S(2)}, u32[]{:S(2)}) collective-permute-start(f16[32,1024]{1,0:T(8,128)(2,1)S(1)} %convert_element_type.36), channel_id=1, source_target_pairs={{0,1},{1,0},{2,3},{3,2},{4,5},{5,4},{6,7},{7,6},{8,9},{9,8},{10,11... | collective-permute-start | bytes 196616 | tf_op jit(solution)/shard_map/ppermute | solution.py:415
  18.4 5.2 %collective-permute-start.6 = (f16[32,1024]{1,0:T(8,128)(2,1)S(1)}, f16[32,1024]{1,0:T(8,128)(2,1)S(1)}, u32[]{:S(2)}, u32[]{:S(2)}) collective-permute-start(f16[32,1024]{1,0:T(8,128)(2,1)S(1)} %convert_element_type.42), channel_id=1, source_target_pairs={{0,4},{1,5},{2,6},{3,7},{4,0},{5,1},{6,2},{7,3},{8,12},{9,13},{10,... | collective-permute-start | bytes 196616 | tf_op jit(solution)/shard_map/ppermute | solution.py:415
  23.7 5.1 %collective-permute-start.9 = (bf16[32,896]{1,0:T(8,128)(2,1)S(1)}, bf16[32,896]{1,0:T(8,128)(2,1)S(1)}, u32[]{:S(2)}, u32[]{:S(2)}) collective-permute-start(bf16[32,896]{1,0:T(8,128)(2,1)S(1)} %combine.3.params0), channel_id=1, source_target_pairs={{0,3},{1,2},{2,1},{3,0},{4,7},{5,6},{6,5},{7,4},{8,11},{9,10},{10,... | collective-permute-start | bytes 172040 | tf_op jit(solution)/shard_map/ppermute | solution.py:415
  25.3 4.2 %collective-permute-start.8 = (bf16[32,896]{1,0:T(8,128)(2,1)S(1)}, bf16[32,896]{1,0:T(8,128)(2,1)S(1)}, u32[]{:S(2)}, u32[]{:S(2)}) collective-permute-start(bf16[32,896]{1,0:T(8,128)(2,1)S(1)} %combine.3.params0), channel_id=1, source_target_pairs={{0,2},{1,3},{2,0},{3,1},{4,6},{5,7},{6,4},{7,5},{8,10},{9,11},{10,... | collective-permute-start | bytes 172040 | tf_op jit(solution)/shard_map/ppermute | solution.py:415
  25.7 4.2 %collective-permute-start.7 = (bf16[32,896]{1,0:T(8,128)(2,1)S(1)}, bf16[32,896]{1,0:T(8,128)(2,1)S(1)}, u32[]{:S(2)}, u32[]{:S(2)}) collective-permute-start(bf16[32,896]{1,0:T(8,128)(2,1)S(1)} %combine.3.params0), channel_id=1, source_target_pairs={{0,1},{1,0},{2,3},{3,2},{4,5},{5,4},{6,7},{7,6},{8,9},{9,8},{10,11... | collective-permute-start | bytes 172040 | tf_op jit(solution)/shard_map/ppermute | solution.py:415
  33.1 1.4 %collective-permute-start.10 = (bf16[2,4,56,76]{3,2,1,0:T(8,128)(2,1)S(1)}, bf16[2,4,56,76]{3,2,1,0:T(8,128)(2,1)S(1)}, u32[]{:S(2)}, u32[]{:S(2)}) collective-permute-start(bf16[2,4,56,76]{3,2,1,0:T(8,128)(2,1)S(1)} %get-tuple-element.31), channel_id=1, source_target_pairs={{0,8},{8,0},{16,24},{24,16},{1,9},{9,1},{17,25},{25,17},{2,10},{10... | collective-permute-start | bytes 204296 | tf_op jit(solution)/shard_map/ppermute | solution.py:415
  34.5 4.2 %collective-permute-start.11 = (bf16[4,56,76]{2,1,0:T(8,128)(2,1)S(1)}, bf16[4,56,76]{2,1,0:T(8,128)(2,1)S(1)}, u32[]{:S(2)}, u32[]{:S(2)}) collective-permute-start(bf16[4,56,76]{2,1,0:T(8,128)(2,1)S(1)} %fusion.1), channel_id=1, source_target_pairs={{0,16},{8,24},{16,0},{24,8},{1,17},{9,25},{17,1},{25,9},{2,18},{10... | collective-permute-start | bytes 102152 | tf_op jit(solution)/shard_map/ppermute | solution.py:415
